TPU v7x, 32 devices: a whole 2x2x4 slice. The times are simulated.
32 devices in a mesh: rows: 8 (over z, x), wide: 4 (over y, core).
Axes of the slice: x: 2, y: 2, z: 4, core: 2. Of those that a mesh axis runs over, the one named last changes fastest.
Arguments:
- hidden_in: bfloat16 [1024, 16, 1024], P('wide', 'rows'), may hold values from -6 to 6
- segments: int32 [16, 1024], P('rows'), may hold values from 0 to 3, never falling along the last dimension, each value on 1 to 768 neighbouring positions
- prefix_vis: int32 [16, 64], P('rows'), may hold values 0 or 1
- prefix_key: bfloat16 [64, 1024], replicated, may hold values from -6 to 6
- prefix_value: bfloat16 [64, 1024], replicated, may hold values from -6 to 6
- w_query: bfloat16 [1024, 1024], replicated, may hold values from -0.375 to 0.375
- w_key: bfloat16 [1024, 1024], replicated, may hold values from -0.1875 to 0.1875
- w_value: bfloat16 [1024, 1024], replicated, may hold values from -0.1875 to 0.1875
- w_out: bfloat16 [1024, 1024], replicated, may hold values from -4 to 4
- norm1_gain: float32 [1024], replicated, may hold values from 0.1 to 1.9
- norm1_bias: float32 [1024], replicated, may hold values from -3 to 3
- w_up: bfloat16 [1024, 4096], P(None, 'wide'), may hold values from -0.1875 to 0.1875
- w_down: bfloat16 [4096, 1024], P('wide'), may hold values from -0.09375 to 0.09375
- norm2_gain: float32 [1024], replicated, may hold values from 0.1 to 1.9
- norm2_bias: float32 [1024], replicated, may hold values from -3 to 3
- out_grad: float32 [1024, 16, 1024], P('wide', 'rows'), may hold values from -6 to 6
Outputs:
- block_out: bfloat16 [1024, 16, 1024], P('wide', 'rows')
- input_grad: float32 [1024, 16, 1024], P('wide', 'rows')
- prefix_key_grad: float32 [64, 1024], replicated
- prefix_value_grad: float32 [64, 1024], replicated
Inputs may be any that keep to these rules, and one draw needn't show every extreme that they name: `segments`: in each row the segment ids never fall, and a segment holds at most 768 positions.
All inputs are finite; a program needn't handle non-finite values. No bound on the sum of `prefix_vis` on one device may be relied on, other than what follows from the above.
Results may differ from a plain program's by a relative error of at most 0.014.
The roundings to bfloat16 on the way count: a program that leaves them out, or rounds other values in their place, can miss the bound.
Values may be sent and summed in bfloat16 or wider, within the bound.
A program may use at most 256 MiB of HBM per device.

v0:
```python
import functools

import jax
import jax.numpy as jnp
from jax import lax
from jax.experimental import pallas as pl
from jax.experimental.pallas import tpu as pltpu
from jax.sharding import PartitionSpec as P

E = 64
P_SIZE = 64
SEGS = 4
PAIR = 2 * E
BIG = 1e30
norm_eps = 1e-05
root_half = 0.7071067811865476
inv_root_tau = 0.3989422804014327

BF = jnp.bfloat16
F32 = jnp.float32
MESH = pl.DeviceIdType.MESH
ANY = pl.BlockSpec(memory_space=pl.ANY)
VM = pl.BlockSpec(memory_space=pltpu.VMEM)
NN = (((1,), (0,)), ((), ()))
NT = (((1,), (1,)), ((), ()))
VMEM_LIMIT = 66 * 1024 * 1000


def dot(a, b, dims=NN):
    return lax.dot_general(a, b, dims, preferred_element_type=F32)


def lanes():
    return lax.broadcasted_iota(jnp.int32, (1, PAIR), 1)


def place():
    row, wide = lax.axis_index("rows"), lax.axis_index("wide")
    return row, wide, lax.rem(wide, 2), lax.div(wide, 2)


def greet(devices):
    barrier = pltpu.get_barrier_semaphore()
    for dev in devices:
        pl.semaphore_signal(barrier, inc=1, device_id=dev, device_id_type=MESH)
    pl.semaphore_wait(barrier, len(devices))


def remote(src, dst, send, recv, dev):
    return pltpu.make_async_remote_copy(
        src_ref=src, dst_ref=dst, send_sem=send, recv_sem=recv, device_id=dev, device_id_type=MESH
    )


def ring_pos(row, rows):
    half = rows // 2
    z, x = lax.div(row, 2), lax.rem(row, 2)
    return z + x * (2 * half - 1 - 2 * z)


def ring_row(pos, rows):
    pos = lax.rem(pos + 2 * rows, rows)
    upper = lax.div(pos, rows // 2)
    return 2 * pos + upper * (2 * rows - 1 - 4 * pos)


def mean_of(value):
    return jnp.mean(value, axis=-1, keepdims=True)


def forward_kernel(
    rows, chips,
    x_own, segs, vis, wq, wk, wv, pkey, pval, w_out, w_up, w_dn, og, g1, b1, g2, b2,
    q_o, ka_o, va_o, kb_o, vb_o, pa_o, pb_o, ra_o, rb_o, mix_o, block_o, gsum_o, gatt_o,
    xbuf, up, dn, wo, mixtok, la, ma, mix_s, ogs, gst,
    load_sem, out_sem, p_sem, x_send, x_recv, y_send, y_recv, d_send, d_recv, f_sem, o_sem,
    mx_send, mx_recv, g_send, g_recv, e_send, e_recv, sh_send, sh_recv, r_send, r_recv, k_send, k_recv,
    l_send, l_recv, gm_send, gm_recv,
):
    batch, per, width = x_own.shape
    tpc = 2 * per
    rem = (chips - 1) * tpc
    keys_b = rem + P_SIZE
    half = width // 2
    pairs = half // PAIR
    hidden = up.shape[3]
    tokens = batch * per
    row, wide, core, chip = place()
    partner = (row, wide + 1 - 2 * core)
    pos = ring_pos(row, rows)
    nxt = (ring_row(pos + 1, rows), wide)
    prv = (ring_row(pos - 1, rows), wide)
    peers = [(row, 2 * lax.rem(chip - d + chips, chips) + core) for d in range(1, chips)]
    mats = ((w_up, up), (w_dn, dn))
    cw = (rows // 2, 2)
    ccw = (rows // 2 - 1, 2)

    col = pl.multiple_of(core * half, half)
    far_loads = [
        pltpu.make_async_copy(w_up, up.at[0, core], load_sem.at[0]),
        pltpu.make_async_copy(w_dn, dn.at[0, core], load_sem.at[1]),
        pltpu.make_async_copy(w_out, wo, load_sem.at[2]),
    ] + [pltpu.make_async_copy(og.at[r], ogs.at[r], load_sem.at[3 + r]) for r in range(batch)]
    x_load = pltpu.make_async_copy(x_own, xbuf.at[:, 0, core], load_sem.at[3 + batch])

    x_pair = remote(x_own, xbuf.at[:, 0, core], x_send, x_recv, partner)
    cross = [
        [
            remote(x_own.at[r], xbuf.at[r, d, core], y_send.at[r, d - 1], y_recv.at[r, d - 1], peers[d - 1])
            for d in range(1, chips)
        ]
        for r in range(batch)
    ]

    def piece(ref, row_at):
        size = ref.shape[-2] // rows
        return pl.ds(pl.multiple_of(row_at * size, size), size)

    def w_cross(m, at, send, recv):
        src, dst = mats[m]
        at = piece(src, at)
        return [
            remote(src.at[at], dst.at[d, core, at], send.at[d - 1], recv.at[d - 1], peers[d - 1])
            for d in range(1, chips)
        ]

    wcross = [w_cross(m, row, g_send.at[m], g_recv.at[m]) for m in range(2)]
    extras = [
        w_cross(1, ring_row(pos + o, rows), e_send.at[o], e_recv.at[o]) for o in range(ccw[1] + 1, rows - cw[1])
    ]
    shards = [
        remote(mats[m][0], mats[m][1].at[0, core], sh_send.at[m], sh_recv.at[m], partner) for m in range(2)
    ]

    def place_of(s, way):
        return ring_row(pos - s if way == 0 else pos + s, rows)

    def ring_copy(m, s, way):
        buf = mats[m][1]
        ref = buf.at[1:, core, piece(buf, place_of(s - 1, way))]
        return remote(ref, ref, r_send.at[m, s, way], r_recv.at[m, s, way], nxt if way == 0 else prv)

    def hand_over(m, s, way):
        buf = mats[m][1]
        ref = buf.at[1:, core, piece(buf, place_of(s, way))]
        return remote(ref, ref, k_send.at[m, s, way], k_recv.at[m, s, way], partner)

    def ways(m, s):
        return range(2 if s <= ccw[m] else 1)

    def hop(m, s):
        if s > cw[m] + 1:
            return
        if s == 1:
            for copy in wcross[m]:
                copy.wait_recv()
            hand_over(m, 0, 0).start()
        else:
            for way in ways(m, s - 1):
                ring_copy(m, s - 1, way).wait_recv()
                hand_over(m, s - 1, way).start()
        if s <= cw[m]:
            for way in ways(m, s):
                ring_copy(m, s, way).start()

    def extra_over(o):
        buf = mats[1][1]
        ref = buf.at[1:, core, piece(buf, place_of(o, 1))]
        return remote(ref, ref, l_send.at[o], l_recv.at[o], partner)

    def take_extras():
        for i, copies in enumerate(extras):
            for copy in copies:
                copy.wait_recv()
            extra_over(ccw[1] + 1 + i).start()

    def gathered(m):
        hand_over(m, 0, 0).wait_recv()
        for s in range(1, cw[m] + 1):
            for way in ways(m, s):
                hand_over(m, s, way).wait_recv()
        if m == 1:
            for i in range(len(extras)):
                extra_over(ccw[1] + 1 + i).wait_recv()

    def sent(m):
        for copy in wcross[m]:
            copy.wait_send()
        hand_over(m, 0, 0).wait_send()
        for s in range(1, cw[m] + 1):
            for way in ways(m, s):
                ring_copy(m, s, way).wait_send()
                hand_over(m, s, way).wait_send()
        if m == 1:
            for i, copies in enumerate(extras):
                for copy in copies:
                    copy.wait_send()
                extra_over(ccw[1] + 1 + i).wait_send()

    mine_at, other_at = pl.multiple_of(core * per, per), pl.multiple_of((1 - core) * per, per)

    def mix_out(r, p):
        cols = pl.ds(pl.multiple_of(core * half + p * PAIR, PAIR), PAIR)
        dst = mixtok.at[pl.ds(pl.multiple_of(r * per, per), per), cols]
        return (
            remote(mix_s.at[r, p, pl.ds(other_at, per)], dst, mx_send.at[r, p], mx_recv.at[r, p], partner),
            pltpu.make_async_copy(mix_s.at[r, p, pl.ds(mine_at, per)], dst, f_sem.at[r, p]),
        )

    def row_out(r):
        return [
            pltpu.make_async_copy(src.at[r], dst.at[r], o_sem.at[r, i])
            for i, (src, dst) in enumerate(((mix_s, mix_o), (la, ra_o), (ma, rb_o)))
        ]

    def attention(wqkv, pks, pvs, q_s, ka, va, kb, vb, s0, s1, s2, s3, oa, pst_a, pst_b, qe, kea, keb):
        loads = [
            x_load,
            pltpu.make_async_copy(wq.at[:, pl.ds(col, half)], wqkv.at[:, 0:half], load_sem.at[4 + batch]),
            pltpu.make_async_copy(wk.at[:, pl.ds(col, half)], wqkv.at[:, half : 2 * half], load_sem.at[5 + batch]),
            pltpu.make_async_copy(wv.at[:, pl.ds(col, half)], wqkv.at[:, 2 * half : 3 * half], load_sem.at[6 + batch]),
            pltpu.make_async_copy(pkey.at[:, pl.ds(col, half)], pks, load_sem.at[7 + batch]),
            pltpu.make_async_copy(pval.at[:, pl.ds(col, half)], pvs, load_sem.at[8 + batch]),
        ]
        for copy in loads:
            copy.start()
        greet([partner, nxt, prv] + peers)
        x_pair.start()
        for group in [wcross[0]] + cross + [wcross[1]] + extras:
            for copy in group:
                copy.start()
        for copy in shards + far_loads:
            copy.start()

        term = lax.broadcasted_iota(jnp.int32, (PAIR, 1), 0)
        term = jnp.where(term >= E, term - E, term)

        def key_terms(seg):
            off = jnp.where(jnp.logical_and(term < SEGS, seg != term), -BIG, 0.0)
            return off.T.astype(BF)

        for r in range(batch):
            for d in range(chips):
                at = pl.multiple_of(lax.rem(chip + d, chips) * tpc, tpc)
                seg = segs[r : r + 1, pl.ds(at, tpc)]
                if d == 0:
                    kea[r] = key_terms(seg)
                    on = jnp.logical_or(term == SEGS, jnp.logical_and(term < SEGS, seg == term))
                    qe[r] = jnp.where(on, 1.0, 0.0).T.astype(BF)
                else:
                    keb[r, (d - 1) * tpc : d * tpc] = key_terms(seg)
            unseen = jnp.logical_and(term == SEGS, vis[r : r + 1, :] == 0)
            keb[r, rem:] = jnp.where(unseen, -BIG, 0.0).T.astype(BF)

        def project(r, d, cb, with_q):
            x = xbuf[r, d, cb]
            if with_q:
                q = (dot(x, wqkv[:, 0:half]) * 0.125).astype(BF)
                for p in range(pairs):
                    q_s[r, p, pl.ds(pl.multiple_of(cb * per, per), per), :] = q[:, p * PAIR : (p + 1) * PAIR]
            for ref_a, ref_b, at in ((ka, kb, 1), (va, vb, 2)):
                y = dot(x, wqkv[:, at * half : (at + 1) * half]).astype(BF)
                for p in range(pairs):
                    val = y[:, p * PAIR : (p + 1) * PAIR]
                    if with_q:
                        ref_a[r, p, pl.ds(pl.multiple_of(cb * per, per), per), :] = val
                    else:
                        ref_b[r, p, pl.ds(pl.multiple_of((d - 1) * tpc + cb * per, per), per), :] = val

        for copy in loads:
            copy.wait()
        for r in range(batch):
            for p in range(pairs):
                kb[r, p, rem:, :] = pks[:, p * PAIR : (p + 1) * PAIR]
                vb[r, p, rem:, :] = pvs[:, p * PAIR : (p + 1) * PAIR]

        @pl.loop(0, 2 * batch)
        def _(i):
            pl.when(i == batch)(x_pair.wait_recv)
            late = lax.div(i, batch)
            project(lax.rem(i, batch), 0, core + late - 2 * core * late, True)

        outs = [
            pltpu.make_async_copy(src, dst, out_sem.at[i])
            for i, (src, dst) in enumerate(((q_s, q_o), (ka, ka_o), (va, va_o), (kb, kb_o), (vb, vb_o)))
        ]
        for copy in outs[:3]:
            copy.start()

        bufs = (s0, s1, s2, s3)

        def score(r, p, h, k_s, kext, buf):
            keys = k_s.shape[2]
            mine = lanes() < E if h == 0 else lanes() >= E
            q = jnp.where(mine, q_s[r, p], qe[r])
            k = jnp.where(mine, k_s[r, p], kext[r])
            buf[:, 0:keys] = dot(q, k, NT)

        def unit(r, p, after, u, k_s, v_s, kext, pst, p_hbm, finish, wait_slot):
            keys = k_s.shape[2]
            copy = pltpu.make_async_copy(pst.at[u], p_hbm.at[r, p], p_sem.at[u])
            pl.when(wait_slot)(copy.wait)
            tops, sums = [], []
            for h in range(2):
                score(after[0], after[1], h, k_s, kext, bufs[2 * (1 - u) + h])
                s = bufs[2 * u + h][:, 0:keys]
                top = jnp.max(s, axis=1, keepdims=True)
                prob = jnp.exp(s - top).astype(BF)
                pst[u, h] = prob
                mine = lanes() < E if h == 0 else lanes() >= E
                v = jnp.where(mine, v_s[r, p], jnp.ones((1, PAIR), BF))
                sums.append(dot(prob, v))
                tops.append(top)
            copy.start()
            low = lanes() < E
            finish(
                r,
                p,
                jnp.where(low, sums[0], sums[1]),
                pltpu.roll(jnp.where(low, sums[1], sums[0]), E, 1),
                jnp.where(low, tops[0], tops[1]),
            )

        def finish_a(r, p, o, l, m):
            oa[r, p], la[r, p], ma[r, p] = o, l, m

        def finish_b(r, p, o, l, m):
            top = jnp.maximum(ma[r, p], m)
            w_a, w_b = jnp.exp(ma[r, p] - top), jnp.exp(m - top)
            inv = 1.0 / (w_a * la[r, p] + w_b * l)
            r_a, r_b = w_a * inv, w_b * inv
            mix_s[r, p] = (oa[r, p] * r_a + o * r_b).astype(BF)
            la[r, p], ma[r, p] = r_a, r_b

        def drain(pst, p_hbm):
            for u in range(2):
                pltpu.make_async_copy(pst.at[u], p_hbm.at[0, 0], p_sem.at[u]).wait()

        args_a = (ka, va, kea, pst_a, pa_o, finish_a)
        for h in range(2):
            score(0, 0, h, ka, kea, bufs[h])
        count = batch * pairs

        @pl.loop(0, count // 2)
        def _(i):
            for u in range(2):
                j = 2 * i + u
                after = jnp.minimum(j + 1, count - 1)
                unit(
                    lax.div(j, pairs), lax.rem(j, pairs), (lax.div(after, pairs), lax.rem(after, pairs)),
                    u, *args_a, i > 0,
                )

            @pl.when(i == 1)
            def _():
                hop(0, 1)

        drain(pst_a, pa_o)
        hop(0, 2)

        args_b = (kb, vb, keb, pst_b, pb_o, finish_b)

        @pl.loop(0, batch)
        def _(r):
            for d in range(1, chips):
                remote(
                    x_own.at[r], xbuf.at[r, d, core], y_send.at[r, d - 1], y_recv.at[r, d - 1], peers[d - 1]
                ).wait_recv()
            forward = remote(
                xbuf.at[r, 1:, core], xbuf.at[r, 1:, core], d_send.at[r], d_recv.at[r], partner
            )
            forward.start()

            @pl.loop(0, 2 * (chips - 1))
            def _(i):
                pl.when(i == chips - 1)(forward.wait_recv)
                late = lax.div(i, chips - 1)
                project(r, lax.rem(i, chips - 1) + 1, core + late - 2 * core * late, False)

            for h in range(2):
                score(r, 0, h, kb, keb, bufs[h])

            @pl.loop(0, pairs // 2)
            def _(i):
                for u in range(2):
                    p = 2 * i + u
                    unit(r, p, (r, jnp.minimum(p + 1, pairs - 1)), u, *args_b, i > 0)
                for step in range(batch):

                    @pl.when(jnp.logical_and(r == step, i == 0))
                    def _(step=step):
                        hop(0, 3 + step)

            drain(pst_b, pb_o)
            for p in range(pairs):
                for copy in mix_out(r, p):
                    copy.start()
            for copy in row_out(r):
                copy.start()
            forward.wait_send()

        for copy in outs[3:]:
            copy.start()
        for s in range(3 + batch, cw[0] + 2):
            hop(0, s)
        hop(1, 1)
        x_pair.wait_send()
        for copy in outs:
            copy.wait()

    vm = pltpu.VMEM
    keys = max(tpc, keys_b)
    pl.run_scoped(
        attention,
        vm((width, 3 * half), BF),
        vm((P_SIZE, half), BF),
        vm((P_SIZE, half), BF),
        vm((batch, pairs, tpc, PAIR), BF),
        vm((batch, pairs, tpc, PAIR), BF),
        vm((batch, pairs, tpc, PAIR), BF),
        vm((batch, pairs, keys_b, PAIR), BF),
        vm((batch, pairs, keys_b, PAIR), BF),
        *([vm((tpc, keys), F32)] * 4),
        vm((batch, pairs, tpc, PAIR), F32),
        vm((2, 2, tpc, tpc), BF),
        vm((2, 2, tpc, keys_b), BF),
        vm((batch, tpc, PAIR), BF),
        vm((batch, tpc, PAIR), BF),
        vm((batch, keys_b, PAIR), BF),
    )

    tile = min(512, hidden)
    tiles = hidden // tile
    total = 2 * chips * tiles
    chunk = 64

    def feed_forward(n1, n1l, sc1, inv1, acc, slope, pre0, pre1, gt, gtl, bst):
        for copy in far_loads:
            copy.wait()
        for r in range(batch):
            for p in range(pairs):
                for copy in mix_out(r, p):
                    copy.wait()

        @pl.loop(0, width // 256)
        def _(j):
            at = pl.ds(pl.multiple_of(j * 256, 256), 256)
            acc[:, at] = dot(mixtok[...], wo[:, at])

        def by_rows(body):
            for r in range(batch):

                @pl.loop(0, per // chunk)
                def _(i, r=r):
                    inner = pl.ds(pl.multiple_of(i * chunk, chunk), chunk)
                    body(r, inner, pl.ds(pl.multiple_of(r * per + i * chunk, chunk), chunk))

        def norm_one(r, inner, at):
            z = acc[at] + xbuf[r, 0, core, inner].astype(F32)
            c = z - mean_of(z)
            inv = lax.rsqrt(mean_of(c * c) + norm_eps)
            s = c * inv
            n = s * g1[...] + b1[...]
            n1[at], n1l[at], sc1[at], inv1[at] = n, n.astype(BF), s, inv
            acc[at] = jnp.zeros_like(z)

        by_rows(norm_one)
        for copy in shards:
            copy.wait()

        def split(j):
            slot = lax.div(j, tiles)
            at = pl.ds(pl.multiple_of(lax.rem(j, tiles) * tile, tile), tile)
            return lax.div(slot, 2), lax.rem(slot, 2), at

        def up_tile(j, buf):
            d, c, at = split(j)
            buf[...] = dot(n1l[...], up[d, c, :, at])

        pres = (pre0, pre1)
        up_tile(0, pre0)

        @pl.loop(0, total // 2)
        def _(i):
            @pl.when(i == tiles - 1)
            def _():
                gathered(0)
                hop(1, 2)

            @pl.when(i == tiles)
            def _():
                take_extras()
                hop(1, 3)
                gathered(1)

            for u in range(2):
                j = 2 * i + u
                up_tile(jnp.minimum(j + 1, total - 1), pres[1 - u])
                v = pres[u][...]
                cdf = 0.5 * (1.0 + lax.erf(v * root_half))
                a = (v * cdf).astype(BF)
                d, c, at = split(j)
                slope[j] = cdf + v * jnp.exp(-0.5 * v * v) * inv_root_tau
                acc[...] += dot(a, dn[d, c, at, :])

        def norm_two(r, inner, at):
            z = n1[at] + acc[at]
            c = z - mean_of(z)
            inv = lax.rsqrt(mean_of(c * c) + norm_eps)
            s = c * inv
            bst[at] = (s * g2[...] + b2[...]).astype(BF)
            t = ogs[r, inner] * g2[...]
            g = inv * (t - mean_of(t) - s * mean_of(t * s))
            gt[at], gtl[at] = g, g.astype(BF)
            acc[at] = jnp.zeros_like(z)

        by_rows(norm_two)
        outs = [
            pltpu.make_async_copy(bst.at[r * per : (r + 1) * per], block_o.at[r], out_sem.at[r])
            for r in range(batch)
        ]
        for copy in outs:
            copy.start()

        def down_back(j, buf):
            d, c, at = split(j)
            buf[...] = dot(gtl[...], dn[d, c, at, :], NT)

        down_back(0, pre0)

        @pl.loop(0, total // 2)
        def _(i):
            for u in range(2):
                j = 2 * i + u
                down_back(jnp.minimum(j + 1, total - 1), pres[1 - u])
                g = (pres[u][...] * slope[j]).astype(BF)
                d, c, at = split(j)
                acc[...] += dot(g, up[d, c, :, at], NT)

        def norm_back(r, inner, at):
            t = (gt[at] + acc[at]) * g1[...]
            s = sc1[at]
            g = inv1[at] * (t - mean_of(t) - s * mean_of(t * s))
            gt[at], gtl[at] = g, g.astype(BF)

        by_rows(norm_back)
        for r in range(batch):
            copy = pltpu.make_async_copy(gt.at[r * per : (r + 1) * per], gsum_o.at[r], out_sem.at[batch + r])
            copy.start()
            outs.append(copy)

        mine = pl.ds(mine_at, per)
        for side in range(2):
            base = (1 - core) * half if side == 0 else core * half
            g = dot(gtl[...], wo[pl.ds(pl.multiple_of(base, half), half), :], NT).astype(BF)
            for p in range(pairs):
                gst[side, p] = g[:, p * PAIR : (p + 1) * PAIR]
            for p in range(pairs):
                for r in range(batch):
                    src, dst = gst.at[side, p, r * per : (r + 1) * per], gatt_o.at[r, p, mine]
                    if side == 0:
                        copy = remote(src, dst, gm_send.at[r, p], gm_recv.at[r, p], partner)
                    else:
                        copy = pltpu.make_async_copy(src, dst, f_sem.at[r, p])
                    copy.start()
                    outs.append(copy)
        for r in range(batch):
            for copy in cross[r]:
                copy.wait_send()
            for copy in row_out(r):
                copy.wait()
        for m in range(2):
            sent(m)
        for copy in outs:
            copy.wait()

    pl.run_scoped(
        feed_forward,
        vm((tokens, width), F32),
        vm((tokens, width), BF),
        vm((tokens, width), F32),
        vm((tokens, 1), F32),
        vm((tokens, width), F32),
        vm((total, tokens, tile), F32),
        vm((tokens, tile), F32),
        vm((tokens, tile), F32),
        vm((tokens, width), F32),
        vm((tokens, width), BF),
        vm((tokens, width), BF),
    )


def forward_call(rows, chips, x, segs, vis, wq, wk, wv, pkey, pval, w_out, w_up, w_dn, og, g1, b1, g2, b2):
    batch, per, width = x.shape
    tpc, half = 2 * per, width // 2
    keys_b = (chips - 1) * tpc + P_SIZE
    pairs = half // PAIR
    tokens = batch * per
    steps = rows // 2
    out = lambda dt, *s: jax.ShapeDtypeStruct(s, dt)
    shapes = (
        out(BF, batch, pairs, tpc, PAIR),
        out(BF, batch, pairs, tpc, PAIR),
        out(BF, batch, pairs, tpc, PAIR),
        out(BF, batch, pairs, keys_b, PAIR),
        out(BF, batch, pairs, keys_b, PAIR),
        out(BF, batch, pairs, 2, tpc, tpc),
        out(BF, batch, pairs, 2, tpc, keys_b),
        out(F32, batch, pairs, tpc, PAIR),
        out(F32, batch, pairs, tpc, PAIR),
        out(BF, batch, pairs, tpc, PAIR),
        out(BF, batch, per, width),
        out(F32, batch, per, width),
        out(BF, batch, pairs, tpc, PAIR),
    )
    dma = pltpu.SemaphoreType.DMA
    vm = pltpu.VMEM
    scratch = [
        vm((batch, chips, 2, per, width), BF),
        vm((chips, 2, *w_up.shape), BF),
        vm((chips, 2, *w_dn.shape), BF),
        vm((width, width), BF),
        vm((tokens, width), BF),
        vm((batch, pairs, tpc, PAIR), F32),
        vm((batch, pairs, tpc, PAIR), F32),
        vm((batch, pairs, tpc, PAIR), BF),
        vm((batch, per, width), F32),
        vm((2, pairs, tokens, PAIR), BF),
        dma((9 + batch,)), dma((5,)), dma((2,)), dma, dma,
        dma((batch, chips - 1)), dma((batch, chips - 1)),
        dma((batch,)), dma((batch,)),
        dma((batch, pairs)), dma((batch, 3)),
        dma((batch, pairs)), dma((batch, pairs)),
        dma((2, chips - 1)), dma((2, chips - 1)),
        dma((rows, chips - 1)), dma((rows, chips - 1)),
        dma((2,)), dma((2,)),
        dma((2, steps + 1, 2)), dma((2, steps + 1, 2)),
        dma((2, steps + 1, 2)), dma((2, steps + 1, 2)),
        dma((rows,)), dma((rows,)),
        dma((batch, pairs)), dma((batch, pairs)),
    ]
    return pl.pallas_call(
        functools.partial(forward_kernel, rows, chips),
        out_shape=shapes,
        in_specs=[ANY] + [VM] * 2 + [ANY] * 9 + [VM] * 4,
        out_specs=[ANY] * len(shapes),
        scratch_shapes=scratch,
        compiler_params=pltpu.CompilerParams(
            collective_id=0, has_side_effects=True, vmem_limit_bytes=VMEM_LIMIT
        ),
        name="forward_and_ffn",
    )(x, segs, vis, wq, wk, wv, pkey, pval, w_out, w_up, w_dn, og, g1, b1, g2, b2)


def backward_kernel(
    rows, chips,
    g_i, mix_i, ra_i, rb_i, q_i, ka_i, va_i, kb_i, vb_i, pa_i, pb_i, wq, wk, wv, gs_i,
    ig_o, pk_o, pv_o,
    g_s, mix_s, ra, rb, q_s, ka, va, kb, vb, w_s, gs, pin_a, pin_b, s0, s1, s2, s3, do0, do1,
    dq, dks, dvs, psum, half_b, send_b, got_b, y_out, y_in, half_a, send_a, got_a,
    pr_in, pr_y, p_full,
    load_sem, p_sem, o_sem, db_send, db_recv, y_send, y_recv, da_send, da_recv,
    p1_send, p1_recv, p2_send, p2_recv, p3_send, p3_recv, p4_send, p4_recv,
):
    batch, pairs, tpc = q_s.shape[0], q_s.shape[1], q_s.shape[2]
    per = tpc // 2
    rem = (chips - 1) * tpc
    width, half = w_s.shape[1], w_s.shape[2]
    row, wide, core, chip = place()
    partner = (row, wide + 1 - 2 * core)
    peers = [(row, 2 * lax.rem(chip - d + chips, chips) + core) for d in range(1, chips)]
    back = [(row, 2 * lax.rem(chip + d, chips) + core) for d in range(1, chips)]
    plane = [(lax.rem(row + t, rows), wide) for t in range(1, rows)]

    col = pl.multiple_of(core * half, half)
    pairs_of = (
        (g_i, g_s), (mix_i, mix_s), (rb_i, rb), (kb_i, kb), (vb_i, vb), (q_i, q_s),
        (wk.at[:, pl.ds(col, half)], w_s.at[1]), (wv.at[:, pl.ds(col, half)], w_s.at[2]),
        (ra_i, ra), (ka_i, ka), (va_i, va), (wq.at[:, pl.ds(col, half)], w_s.at[0]), (gs_i, gs),
    )
    loads = [pltpu.make_async_copy(src, dst, load_sem.at[i]) for i, (src, dst) in enumerate(pairs_of)]

    def fetch(pin, p_hbm, r, p, u):
        return pltpu.make_async_copy(p_hbm.at[r, p], pin.at[u], p_sem.at[u])

    for copy in loads[:6]:
        copy.start()
    for u in range(2):
        fetch(pin_b, pb_i, 0, u, u).start()
    for copy in loads[6:]:
        copy.start()
    greet([partner] + peers + plane)
    for copy in loads[:6]:
        copy.wait()

    bufs, dos = (s0, s1, s2, s3), (do0, do1)

    def first(r, p, u, v_s, scale):
        keys = v_s.shape[2]
        g = g_s[r, p].astype(F32) * scale[r, p]
        do = g.astype(BF)
        dos[u][...] = do
        t = g * mix_s[r, p].astype(F32)
        lane = lanes()
        for h in range(2):
            mine = lane < E if h == 0 else lane >= E
            delta = jnp.sum(jnp.where(mine, t, 0.0), axis=1, keepdims=True)
            hi = delta.astype(BF)
            left = delta - hi.astype(F32)
            mid = left.astype(BF)
            low = (left - mid.astype(F32)).astype(BF)
            at = E if h == 0 else 0
            ext = jnp.where(
                lane == at, -hi, jnp.where(lane == at + 1, -mid, jnp.where(lane == at + 2, -low, jnp.zeros((1, PAIR), BF)))
            )
            one = jnp.where(jnp.logical_and(lane >= at, lane < at + 3), 1.0, 0.0).astype(BF)
            bufs[2 * u + h][:, 0:keys] = dot(
                jnp.where(mine, do, ext), jnp.where(mine, v_s[r, p], one), NT
            )

    def second(r, p, u, k_s, pin, start_dq, prefix):
        keys = k_s.shape[2]
        q2, k2, do = q_s[r, p], k_s[r, p], dos[u][...]
        do_t, q_t = do.T, q2.T
        gq, gk, gv = [], [], []
        for h in range(2):
            prob = pin[u, h]
            ds = (prob.astype(F32) * bufs[2 * u + h][:, 0:keys]).astype(BF)
            at = slice(h * E, (h + 1) * E)
            gv.append(dot(do_t[at], prob))
            gk.append(dot(q_t[at], ds))
            gq.append(dot(ds, k2))
        low = lanes() < E
        grad = jnp.where(low, gq[0], gq[1])
        dq[r, p] = grad if start_dq else dq[r, p] + grad
        cols = pl.ds(pl.multiple_of(p * PAIR, PAIR), PAIR)
        for ref, parts, k in ((dks, gk, 0), (dvs, gv, 1)):
            val = jnp.concatenate(parts, axis=0).T
            if prefix:
                ref[0:rem, cols] = val[:rem].astype(BF)
                psum[k * P_SIZE : (k + 1) * P_SIZE, cols] += val[rem:]
            else:
                ref[0:tpc, cols] = val.astype(BF)

    def group(r, k_s, v_s, scale, pin, p_hbm, start_dq, prefix):
        first(r, 0, 0, v_s, scale)

        @pl.loop(0, pairs // 2)
        def _(i):
            for u in range(2):
                p = 2 * i + u
                fetch(pin, p_hbm, r, p, u).wait()
                first(r, jnp.minimum(p + 1, pairs - 1), 1 - u, v_s, scale)
                second(r, p, u, k_s, pin, start_dq, prefix)

                @pl.when(i < pairs // 2 - 1)
                def _():
                    fetch(pin, p_hbm, r, p + 2, u).start()

    def to_inputs(at):
        keys = dot(dks[at], w_s[1], NT)
        return keys + dot(dvs[at], w_s[2], NT)

    psum[...] = jnp.zeros_like(psum)
    tails = []
    y_copies = []
    b_copies = []

    def chip_sum(r):
        for copy in b_copies[r]:
            copy.wait_recv()
        for d in range(1, chips):
            y_out[r, d - 1] = (half_b[r, d - 1] + got_b[r, d - 1]).astype(BF)
        copies = [
            remote(
                y_out.at[r, d - 1], y_in.at[r, d - 1], y_send.at[r, d - 1], y_recv.at[r, d - 1], back[d - 1]
            )
            for d in range(1, chips)
        ]
        for copy in copies:
            copy.start()
        y_copies.append(copies)

    for r in range(batch):
        group(r, kb, vb, rb, pin_b, pb_i, True, True)
        if r + 1 < batch:
            for u in range(2):
                fetch(pin_b, pb_i, r + 1, u, u).start()
        else:
            for u in range(2):
                fetch(pin_a, pa_i, 0, u, u).start()
        if r == 0:
            for copy in loads[6:]:
                copy.wait()
        copies = []
        for d in range(1, chips):
            at = pl.ds(pl.multiple_of((d - 1) * tpc + (1 - core) * per, per), per)
            send_b[r, d - 1] = to_inputs(at)
            copy = remote(
                send_b.at[r, d - 1], got_b.at[r, d - 1], db_send.at[r, d - 1], db_recv.at[r, d - 1], partner
            )
            copy.start()
            copies.append(copy)
        b_copies.append(copies)
        for d in range(1, chips):
            at = pl.ds(pl.multiple_of((d - 1) * tpc + core * per, per), per)
            half_b[r, d - 1] = to_inputs(at)
        chip_sum(r)

    size = 2 * P_SIZE // rows

    def part(at):
        return pl.ds(pl.multiple_of(at * size, size), size)

    p_one = [
        remote(psum.at[part(plane[t - 1][0])], pr_in.at[t - 1], p1_send.at[t - 1], p1_recv.at[t - 1], plane[t - 1])
        for t in range(1, rows)
    ]
    for copy in p_one:
        copy.start()

    for r in range(batch):
        group(r, ka, va, ra, pin_a, pa_i, False, False)
        if r + 1 < batch:
            for u in range(2):
                fetch(pin_a, pa_i, r + 1, u, u).start()
        for side in range(2):
            block = pl.multiple_of(((1 - core) if side == 0 else core) * per, per)
            at = pl.ds(block, per)
            part_in = to_inputs(at)
            for p in range(pairs):
                dvs[at, p * PAIR : (p + 1) * PAIR] = (dq[r, p, at, :]).astype(BF)
            val = part_in + 0.125 * dot(dvs[at], w_s[0], NT)
            if side == 0:
                send_a[r] = val
                copy = remote(send_a.at[r], got_a.at[r], da_send.at[r], da_recv.at[r], partner)
                copy.start()
                tails.append(copy)
            else:
                half_a[r] = gs[r] + val
        if r == 0:
            for copy in p_one:
                copy.wait_recv()
            total = psum[part(row)]
            for t in range(1, rows):
                total = total + pr_in[t - 1]
            pr_y[0] = total
            p_two = [
                remote(pr_y.at[0], pr_y.at[d], p2_send.at[d - 1], p2_recv.at[d - 1], peers[d - 1])
                for d in range(1, chips)
            ]
            for copy in p_two:
                copy.start()
        if r == batch - 1:
            for copy in p_two:
                copy.wait()
            whole = jnp.zeros((size, half), F32)
            for c in range(chips):
                whole = whole + pr_y[lax.rem(c - chip + chips, chips)]
            p_full[part(row)] = whole
            p_three = [
                remote(p_full.at[part(row)], p_full.at[part(row)], p3_send.at[t - 1], p3_recv.at[t - 1], plane[t - 1])
                for t in range(1, rows)
            ]
            for copy in p_three:
                copy.start()

    outs = []
    for r in range(batch):
        tails[r].wait()
        for copy in y_copies[r]:
            copy.wait()
        val = half_a[r] + got_a[r]
        for d in range(1, chips):
            val = val + y_in[r, d - 1].astype(F32)
        half_a[r] = val
        copy = pltpu.make_async_copy(half_a.at[r], ig_o.at[r], o_sem.at[r])
        copy.start()
        outs.append(copy)
    for copy in p_three:
        copy.wait()
    cols = pl.ds(col, half)
    for k, ref in enumerate((pk_o, pv_o)):
        src = p_full.at[k * P_SIZE : (k + 1) * P_SIZE]
        copy = remote(src, ref.at[:, cols], p4_send.at[k], p4_recv.at[k], partner)
        copy.start()
        outs.append(copy)
        copy = pltpu.make_async_copy(src, ref.at[:, cols], o_sem.at[batch + k])
        copy.start()
        outs.append(copy)
    for copies in b_copies:
        for copy in copies:
            copy.wait_send()
    for copy in p_one:
        copy.wait_send()
    for copy in outs:
        copy.wait()


def backward_call(rows, chips, g, mix, ra, rb, q, ka, va, kb, vb, pa, pb, wq, wk, wv, gs):
    batch, pairs, tpc, _ = q.shape
    keys_a, keys_b = ka.shape[2], kb.shape[2]
    per, width = gs.shape[1], gs.shape[2]
    half = width // 2
    size = 2 * P_SIZE // rows
    out = lambda dt, *s: jax.ShapeDtypeStruct(s, dt)
    dma = pltpu.SemaphoreType.DMA
    vm = pltpu.VMEM
    far = chips - 1
    keys = max(keys_a, keys_b)
    return pl.pallas_call(
        functools.partial(backward_kernel, rows, chips),
        out_shape=(
            out(F32, batch, per, width),
            out(F32, P_SIZE, width),
            out(F32, P_SIZE, width),
        ),
        in_specs=[ANY] * 15,
        out_specs=[ANY] * 3,
        scratch_shapes=[
            vm((batch, pairs, tpc, PAIR), BF),
            vm((batch, pairs, tpc, PAIR), BF),
            vm((batch, pairs, tpc, PAIR), F32),
            vm((batch, pairs, tpc, PAIR), F32),
            vm((batch, pairs, tpc, PAIR), BF),
            vm((batch, pairs, keys_a, PAIR), BF),
            vm((batch, pairs, keys_a, PAIR), BF),
            vm((batch, pairs, keys_b, PAIR), BF),
            vm((batch, pairs, keys_b, PAIR), BF),
            vm((3, width, half), BF),
            vm((batch, per, width), F32),
            vm((2, 2, tpc, keys_a), BF),
            vm((2, 2, tpc, keys_b), BF),
            *([vm((tpc, keys), F32)] * 4),
            *([vm((tpc, PAIR), BF)] * 2),
            vm((batch, pairs, tpc, PAIR), F32),
            vm((keys, half), BF),
            vm((keys, half), BF),
            vm((2 * P_SIZE, half), F32),
            vm((batch, far, per, width), F32),
            vm((batch, far, per, width), F32),
            vm((batch, far, per, width), F32),
            vm((batch, far, per, width), BF),
            vm((batch, far, per, width), BF),
            vm((batch, per, width), F32),
            vm((batch, per, width), F32),
            vm((batch, per, width), F32),
            vm((rows - 1, size, half), F32),
            vm((chips, size, half), F32),
            vm((2 * P_SIZE, half), F32),
            dma((13,)), dma((2,)), dma((batch + 2,)),
            dma((batch, far)), dma((batch, far)),
            dma((batch, far)), dma((batch, far)),
            dma((batch,)), dma((batch,)),
            dma((rows - 1,)), dma((rows - 1,)),
            dma((far,)), dma((far,)),
            dma((rows - 1,)), dma((rows - 1,)),
            dma((2,)), dma((2,)),
        ],
        compiler_params=pltpu.CompilerParams(
            collective_id=2, has_side_effects=True, vmem_limit_bytes=VMEM_LIMIT
        ),
        name="attention_backward",
    )(g, mix, ra, rb, q, ka, va, kb, vb, pa, pb, wq, wk, wv, gs)


def on_device(
    rows, chips,
    hidden_in, segments, prefix_vis, prefix_key, prefix_value, w_query, w_key, w_value, w_out,
    norm1_gain, norm1_bias, w_up, w_down, norm2_gain, norm2_bias, out_grad,
):
    x = jnp.transpose(hidden_in, (1, 0, 2))
    og = jnp.transpose(out_grad, (1, 0, 2))
    flat = lambda v: v.reshape(1, -1)
    q, ka, va, kb, vb, pa, pb, ra, rb, mix, block, gs, g = forward_call(
        rows, chips, x, segments, prefix_vis, w_query, w_key, w_value, prefix_key, prefix_value,
        w_out, w_up, w_down, og, flat(norm1_gain), flat(norm1_bias), flat(norm2_gain), flat(norm2_bias),
    )
    input_grad, pk_grad, pv_grad = backward_call(
        rows, chips, g, mix, ra, rb, q, ka, va, kb, vb, pa, pb, w_query, w_key, w_value, gs
    )
    return (
        jnp.transpose(block, (1, 0, 2)),
        jnp.transpose(input_grad, (1, 0, 2)),
        pk_grad,
        pv_grad,
    )


def solution(mesh):
    rows, chips = mesh.shape["rows"], mesh.shape["wide"] // 2
    act = P("wide", "rows", None)
    per_row = P("rows", None)
    in_specs = (
        act, per_row, per_row, *([P()] * 8), P(None, "wide"), P("wide", None), P(), P(), act,
    )
    out_specs = (act, act, P(), P())
    return jax.shard_map(
        functools.partial(on_device, rows, chips),
        mesh=mesh,
        in_specs=in_specs,
        out_specs=out_specs,
        check_vma=False,
    )
```

profile of v0, /device:TPU:0, one launch (start us, length us, event | category | flops | bytes accessed | tf_op | source)
XLA Modules:
  0.0 152.0 jit_solution(1184693838733875765)
XLA Ops:
  0.6 0.0 copy-start
  0.6 2.6 %copy.27 = bf16[256,2,1024]{2,0,1:T(8,128)(2,1)} copy(bf16[256,2,1024]{2,1,0:T(2,128)(2,1)} %param.16) | data formatting | bytes 2097152 | tf_op args[0]
  3.3 0.0 copy-done
  3.3 2.0 %copy.26 = f32[256,2,1024]{2,0,1:T(8,128)} copy(f32[256,2,1024]{2,1,0:T(2,128)S(1)} %copy-done) | data formatting | bytes 4194304 | tf_op args[15]
  5.2 90.2 %forward_and_ffn.1 = (bf16[2,4,512,128]{3,2,1,0:T(8,128)(2,1)}, bf16[2,4,512,128]{3,2,1,0:T(8,128)(2,1)}, bf16[2,4,512,128]{3,2,1,0:T(8,128)(2,1)}, bf16[2,4,576...) custom-call(bf16[2,256,1024]{2,1,0:T(8,128)(2,1)} %bitcast.13, ...), custom_call_target="tpu_custom_call" | custom-call | tf_op jit(solution)/shard_map/forward_and_ffn/pallas_call | solution.py:642
  95.4 3.3 %copy.22 = bf16[256,2,1024]{2,1,0:T(2,128)(2,1)} copy(bf16[256,2,1024]{2,0,1:T(8,128)(2,1)} %bitcast.15) | data formatting | bytes 2097152
  98.7 47.3 %attention_backward.1 = (f32[2,256,1024]{2,1,0:T(8,128)}, f32[64,1024]{1,0:T(8,128)}, f32[64,1024]{1,0:T(8,128)}) custom-call(bf16[2,4,512,128]{3,2,1,0:T(8,128)(2,1)} %get-tuple-element.21.g_i, bf16[2,4,512,128]{3,2,1,0:T(8,128)(2,1)} %get-tuple-element.22.mix_i, f32[2,4,512,128]{3,2,1,0:T(8,128)} %get-tuple-element.23.ra_i, ...), custom_call_target="tpu_custom_call" | custom-call | tf_op jit(solution)/shard_map/attention_backward/pallas_call | solution.py:911
  146.0 0.0 copy-start.2
  146.0 0.0 copy-start.1
  146.0 4.6 %copy.23 = f32[256,2,1024]{2,1,0:T(2,128)} copy(f32[256,2,1024]{2,0,1:T(8,128)} %bitcast.14) | data formatting | bytes 4194304
  150.6 0.0 copy-done.2
  150.6 0.7 copy.30
  151.3 0.0 copy-done.1
  151.3 0.7 copy.31
Async XLA Ops:
  0.6 2.6 %copy-start = (f32[256,2,1024]{2,1,0:T(2,128)S(1)}, f32[256,2,1024]{2,1,0:T(2,128)}, u32[]{:S(2)}) copy-start(f32[256,2,1024]{2,1,0:T(2,128)} %param.31) | copy-start | bytes 6291460
  146.0 4.6 %copy-start.2 = (f32[64,1024]{1,0:T(8,128)S(1)}, f32[64,1024]{1,0:T(8,128)}, u32[]{:S(2)}) copy-start(f32[64,1024]{1,0:T(8,128)} %get-tuple-element.46) | copy-start | bytes 786436
  146.0 5.3 %copy-start.1 = (f32[64,1024]{1,0:T(8,128)S(1)}, f32[64,1024]{1,0:T(8,128)}, u32[]{:S(2)}) copy-start(f32[64,1024]{1,0:T(8,128)} %get-tuple-element.47) | copy-start | bytes 786436
where the time goes:
time: 152 us
  Pallas kernels  137 us (90%)
  local copies, waits for them, and re-layouts  13.9 us (9%)
    pallas_call x1, Pallas kernels, forward_call(): pl.pallas_call(functools.partial(forward_kernel, rows, chips), out_shape=...  90.2 us
    pallas_call x1, Pallas kernels, backward_call(): pl.pallas_call(functools.partial(backward_kernel, rows, chips), out_shape...  47.3 us
    unnamed x12, local copies, waits for them, and re-layouts  13.9 us

commit v1 on v0

--- a/solution.py
+++ b/solution.py
@@ -77,7 +77,7 @@
     mx_send, mx_recv, g_send, g_recv, e_send, e_recv, sh_send, sh_recv, r_send, r_recv, k_send, k_recv,
     l_send, l_recv, gm_send, gm_recv,
 ):
-    batch, per, width = x_own.shape
+    per, batch, width = x_own.shape
     tpc = 2 * per
     rem = (chips - 1) * tpc
     keys_b = rem + P_SIZE
@@ -92,42 +92,45 @@
     prv = (ring_row(pos - 1, rows), wide)
     peers = [(row, 2 * lax.rem(chip - d + chips, chips) + core) for d in range(1, chips)]
     mats = ((w_up, up), (w_dn, dn))
-    cw = (rows // 2, 2)
-    ccw = (rows // 2 - 1, 2)
+    cw = (rows // 2, 3)
+    ccw = (rows // 2 - 1, 3)
+    cuts = (1, 2 if hidden // rows >= 64 else 1)
 
     col = pl.multiple_of(core * half, half)
     far_loads = [
         pltpu.make_async_copy(w_up, up.at[0, core], load_sem.at[0]),
         pltpu.make_async_copy(w_dn, dn.at[0, core], load_sem.at[1]),
         pltpu.make_async_copy(w_out, wo, load_sem.at[2]),
-    ] + [pltpu.make_async_copy(og.at[r], ogs.at[r], load_sem.at[3 + r]) for r in range(batch)]
-    x_load = pltpu.make_async_copy(x_own, xbuf.at[:, 0, core], load_sem.at[3 + batch])
-
-    x_pair = remote(x_own, xbuf.at[:, 0, core], x_send, x_recv, partner)
+    ] + [pltpu.make_async_copy(og.at[:, r], ogs.at[r], load_sem.at[3 + r]) for r in range(batch)]
+
+    x_pair = remote(xbuf.at[:, 0, core], xbuf.at[:, 0, core], x_send, x_recv, partner)
     cross = [
         [
-            remote(x_own.at[r], xbuf.at[r, d, core], y_send.at[r, d - 1], y_recv.at[r, d - 1], peers[d - 1])
+            remote(xbuf.at[r, 0, core], xbuf.at[r, d, core], y_send.at[r, d - 1], y_recv.at[r, d - 1], peers[d - 1])
             for d in range(1, chips)
         ]
         for r in range(batch)
     ]
 
-    def piece(ref, row_at):
+    def piece(ref, row_at, cut=0, cuts_of=1):
         size = ref.shape[-2] // rows
-        return pl.ds(pl.multiple_of(row_at * size, size), size)
-
-    def w_cross(m, at, send, recv):
+        sub = size // cuts_of
+        return pl.ds(pl.multiple_of(row_at * size + cut * sub, sub), sub)
+
+    def w_cross(m, row_at, cut, cuts_of, send, recv):
         src, dst = mats[m]
-        at = piece(src, at)
+        at = piece(src, row_at, cut, cuts_of)
         return [
             remote(src.at[at], dst.at[d, core, at], send.at[d - 1], recv.at[d - 1], peers[d - 1])
             for d in range(1, chips)
         ]
 
-    wcross = [w_cross(m, row, g_send.at[m], g_recv.at[m]) for m in range(2)]
-    extras = [
-        w_cross(1, ring_row(pos + o, rows), e_send.at[o], e_recv.at[o]) for o in range(ccw[1] + 1, rows - cw[1])
+    split_cross = [
+        [w_cross(m, row, h, cuts[m], g_send.at[m, h], g_recv.at[m, h]) for h in range(cuts[m])] for m in range(2)
     ]
+    wcross = [sum(group, []) for group in split_cross]
+    far_off = range(ccw[1] + 1, rows - cw[1])
+    extras = sum([w_cross(1, ring_row(pos + o, rows), 0, 1, e_send.at[o], e_recv.at[o]) for o in far_off], [])
     shards = [
         remote(mats[m][0], mats[m][1].at[0, core], sh_send.at[m], sh_recv.at[m], partner) for m in range(2)
     ]
@@ -135,33 +138,33 @@
     def place_of(s, way):
         return ring_row(pos - s if way == 0 else pos + s, rows)
 
-    def ring_copy(m, s, way):
+    def ring_copy(m, s, way, h):
         buf = mats[m][1]
-        ref = buf.at[1:, core, piece(buf, place_of(s - 1, way))]
-        return remote(ref, ref, r_send.at[m, s, way], r_recv.at[m, s, way], nxt if way == 0 else prv)
-
-    def hand_over(m, s, way):
+        ref = buf.at[1:, core, piece(buf, place_of(s - 1, way), h, cuts[m])]
+        return remote(ref, ref, r_send.at[m, s, way, h], r_recv.at[m, s, way, h], nxt if way == 0 else prv)
+
+    def hand_over(m, s, way, h):
         buf = mats[m][1]
-        ref = buf.at[1:, core, piece(buf, place_of(s, way))]
-        return remote(ref, ref, k_send.at[m, s, way], k_recv.at[m, s, way], partner)
+        ref = buf.at[1:, core, piece(buf, place_of(s, way), h, cuts[m])]
+        return remote(ref, ref, k_send.at[m, s, way, h], k_recv.at[m, s, way, h], partner)
 
     def ways(m, s):
         return range(2 if s <= ccw[m] else 1)
 
-    def hop(m, s):
-        if s > cw[m] + 1:
+    def hop(m, s, h=0):
+        if s > cw[m] + 1 or h >= cuts[m]:
             return
         if s == 1:
-            for copy in wcross[m]:
+            for copy in split_cross[m][h]:
                 copy.wait_recv()
-            hand_over(m, 0, 0).start()
         else:
             for way in ways(m, s - 1):
-                ring_copy(m, s - 1, way).wait_recv()
-                hand_over(m, s - 1, way).start()
+                ring_copy(m, s - 1, way, h).wait_recv()
         if s <= cw[m]:
             for way in ways(m, s):
-                ring_copy(m, s, way).start()
+                ring_copy(m, s, way, h).start()
+        for way in ways(m, s - 1) if s > 1 else range(1):
+            hand_over(m, s - 1, way, h).start()
 
     def extra_over(o):
         buf = mats[1][1]
@@ -169,33 +172,30 @@
         return remote(ref, ref, l_send.at[o], l_recv.at[o], partner)
 
     def take_extras():
-        for i, copies in enumerate(extras):
-            for copy in copies:
-                copy.wait_recv()
-            extra_over(ccw[1] + 1 + i).start()
+        for copy in extras:
+            copy.wait_recv()
+        for o in far_off:
+            extra_over(o).start()
+
+    def all_over(m):
+        copies = [hand_over(m, 0, 0, h) for h in range(cuts[m])]
+        for s in range(1, cw[m] + 1):
+            copies += [hand_over(m, s, way, h) for way in ways(m, s) for h in range(cuts[m])]
+        if m == 1:
+            copies += [extra_over(o) for o in far_off]
+        return copies
 
     def gathered(m):
-        hand_over(m, 0, 0).wait_recv()
+        for copy in all_over(m):
+            copy.wait_recv()
+
+    def sent(m):
+        for copy in wcross[m] + all_over(m) + (extras if m == 1 else []):
+            copy.wait_send()
         for s in range(1, cw[m] + 1):
             for way in ways(m, s):
-                hand_over(m, s, way).wait_recv()
-        if m == 1:
-            for i in range(len(extras)):
-                extra_over(ccw[1] + 1 + i).wait_recv()
-
-    def sent(m):
-        for copy in wcross[m]:
-            copy.wait_send()
-        hand_over(m, 0, 0).wait_send()
-        for s in range(1, cw[m] + 1):
-            for way in ways(m, s):
-                ring_copy(m, s, way).wait_send()
-                hand_over(m, s, way).wait_send()
-        if m == 1:
-            for i, copies in enumerate(extras):
-                for copy in copies:
-                    copy.wait_send()
-                extra_over(ccw[1] + 1 + i).wait_send()
+                for h in range(cuts[m]):
+                    ring_copy(m, s, way, h).wait_send()
 
     mine_at, other_at = pl.multiple_of(core * per, per), pl.multiple_of((1 - core) * per, per)
 
@@ -213,20 +213,28 @@
             for i, (src, dst) in enumerate(((mix_s, mix_o), (la, ra_o), (ma, rb_o)))
         ]
 
-    def attention(wqkv, pks, pvs, q_s, ka, va, kb, vb, s0, s1, s2, s3, oa, pst_a, pst_b, qe, kea, keb):
+    def attention(wqkv, pks, pvs, q_s, ka, va, kb, vb, s0, s1, s2, s3, oa, pst_a, pst_b, qe, kea, keb, xraw):
+        x_load = pltpu.make_async_copy(x_own, xraw, load_sem.at[3 + batch])
         loads = [
-            x_load,
             pltpu.make_async_copy(wq.at[:, pl.ds(col, half)], wqkv.at[:, 0:half], load_sem.at[4 + batch]),
             pltpu.make_async_copy(wk.at[:, pl.ds(col, half)], wqkv.at[:, half : 2 * half], load_sem.at[5 + batch]),
             pltpu.make_async_copy(wv.at[:, pl.ds(col, half)], wqkv.at[:, 2 * half : 3 * half], load_sem.at[6 + batch]),
             pltpu.make_async_copy(pkey.at[:, pl.ds(col, half)], pks, load_sem.at[7 + batch]),
             pltpu.make_async_copy(pval.at[:, pl.ds(col, half)], pvs, load_sem.at[8 + batch]),
         ]
+        barrier = pltpu.get_barrier_semaphore()
+        friends = [partner, nxt, prv] + peers
+        for dev in friends:
+            pl.semaphore_signal(barrier, inc=1, device_id=dev, device_id_type=MESH)
+        x_load.start()
         for copy in loads:
             copy.start()
-        greet([partner, nxt, prv] + peers)
+        x_load.wait()
+        for r in range(batch):
+            xbuf[r, 0, core] = xraw[:, r, :]
+        pl.semaphore_wait(barrier, len(friends))
         x_pair.start()
-        for group in [wcross[0]] + cross + [wcross[1]] + extras:
+        for group in [wcross[0]] + cross + [wcross[1]] + [extras]:
             for copy in group:
                 copy.start()
         for copy in shards + far_loads:
@@ -351,7 +359,7 @@
                     u, *args_a, i > 0,
                 )
 
-            @pl.when(i == 1)
+            @pl.when(i == 0)
             def _():
                 hop(0, 1)
 
@@ -364,7 +372,7 @@
         def _(r):
             for d in range(1, chips):
                 remote(
-                    x_own.at[r], xbuf.at[r, d, core], y_send.at[r, d - 1], y_recv.at[r, d - 1], peers[d - 1]
+                    xbuf.at[r, 0, core], xbuf.at[r, d, core], y_send.at[r, d - 1], y_recv.at[r, d - 1], peers[d - 1]
                 ).wait_recv()
             forward = remote(
                 xbuf.at[r, 1:, core], xbuf.at[r, 1:, core], d_send.at[r], d_recv.at[r], partner
@@ -377,6 +385,14 @@
                 late = lax.div(i, chips - 1)
                 project(r, lax.rem(i, chips - 1) + 1, core + late - 2 * core * late, False)
 
+            @pl.when(r == 0)
+            def _():
+                hop(0, 3)
+
+            @pl.when(r == 1)
+            def _():
+                hop(1, 1, 0)
+
             for h in range(2):
                 score(r, 0, h, kb, keb, bufs[h])
 
@@ -385,11 +401,14 @@
                 for u in range(2):
                     p = 2 * i + u
                     unit(r, p, (r, jnp.minimum(p + 1, pairs - 1)), u, *args_b, i > 0)
-                for step in range(batch):
-
-                    @pl.when(jnp.logical_and(r == step, i == 0))
-                    def _(step=step):
-                        hop(0, 3 + step)
+                @pl.when(jnp.logical_and(r == 1, i == 0))
+                def _():
+                    hop(0, 5)
+                    hop(1, 1, 1)
+
+                @pl.when(jnp.logical_and(r == 1, i == 1))
+                def _():
+                    hop(1, 2, 0)
 
             drain(pst_b, pb_o)
             for p in range(pairs):
@@ -399,11 +418,14 @@
                 copy.start()
             forward.wait_send()
 
+            @pl.when(r == 0)
+            def _():
+                hop(0, 4)
+
         for copy in outs[3:]:
             copy.start()
-        for s in range(3 + batch, cw[0] + 2):
+        for s in range(6, cw[0] + 2):
             hop(0, s)
-        hop(1, 1)
         x_pair.wait_send()
         for copy in outs:
             copy.wait()
@@ -427,6 +449,7 @@
         vm((batch, tpc, PAIR), BF),
         vm((batch, tpc, PAIR), BF),
         vm((batch, keys_b, PAIR), BF),
+        vm((per, batch, width), BF),
     )
 
     tile = min(512, hidden)
@@ -446,6 +469,8 @@
         def _(j):
             at = pl.ds(pl.multiple_of(j * 256, 256), 256)
             acc[:, at] = dot(mixtok[...], wo[:, at])
+
+        hop(1, 2, 1)
 
         def by_rows(body):
             for r in range(batch):
@@ -465,6 +490,8 @@
             acc[at] = jnp.zeros_like(z)
 
         by_rows(norm_one)
+        hop(1, 3, 0)
+        take_extras()
         for copy in shards:
             copy.wait()
 
@@ -482,15 +509,15 @@
 
         @pl.loop(0, total // 2)
         def _(i):
-            @pl.when(i == tiles - 1)
+            @pl.when(i == max(tiles - 1, 0))
             def _():
                 gathered(0)
-                hop(1, 2)
+                hop(1, 3, 1)
 
             @pl.when(i == tiles)
             def _():
-                take_extras()
-                hop(1, 3)
+                hop(1, 4, 0)
+                hop(1, 4, 1)
                 gathered(1)
 
             for u in range(2):
@@ -508,19 +535,15 @@
             c = z - mean_of(z)
             inv = lax.rsqrt(mean_of(c * c) + norm_eps)
             s = c * inv
-            bst[at] = (s * g2[...] + b2[...]).astype(BF)
+            bst[inner, r, :] = (s * g2[...] + b2[...]).astype(BF)
             t = ogs[r, inner] * g2[...]
             g = inv * (t - mean_of(t) - s * mean_of(t * s))
             gt[at], gtl[at] = g, g.astype(BF)
             acc[at] = jnp.zeros_like(z)
 
         by_rows(norm_two)
-        outs = [
-            pltpu.make_async_copy(bst.at[r * per : (r + 1) * per], block_o.at[r], out_sem.at[r])
-            for r in range(batch)
-        ]
-        for copy in outs:
-            copy.start()
+        outs = [pltpu.make_async_copy(bst, block_o, out_sem.at[0])]
+        outs[0].start()
 
         def down_back(j, buf):
             d, c, at = split(j)
@@ -586,12 +609,12 @@
         vm((tokens, tile), F32),
         vm((tokens, width), F32),
         vm((tokens, width), BF),
-        vm((tokens, width), BF),
+        vm((per, batch, width), BF),
     )
 
 
 def forward_call(rows, chips, x, segs, vis, wq, wk, wv, pkey, pval, w_out, w_up, w_dn, og, g1, b1, g2, b2):
-    batch, per, width = x.shape
+    per, batch, width = x.shape
     tpc, half = 2 * per, width // 2
     keys_b = (chips - 1) * tpc + P_SIZE
     pairs = half // PAIR
@@ -609,7 +632,7 @@
         out(F32, batch, pairs, tpc, PAIR),
         out(F32, batch, pairs, tpc, PAIR),
         out(BF, batch, pairs, tpc, PAIR),
-        out(BF, batch, per, width),
+        out(BF, per, batch, width),
         out(F32, batch, per, width),
         out(BF, batch, pairs, tpc, PAIR),
     )
@@ -631,11 +654,11 @@
         dma((batch,)), dma((batch,)),
         dma((batch, pairs)), dma((batch, 3)),
         dma((batch, pairs)), dma((batch, pairs)),
-        dma((2, chips - 1)), dma((2, chips - 1)),
+        dma((2, 2, chips - 1)), dma((2, 2, chips - 1)),
         dma((rows, chips - 1)), dma((rows, chips - 1)),
         dma((2,)), dma((2,)),
-        dma((2, steps + 1, 2)), dma((2, steps + 1, 2)),
-        dma((2, steps + 1, 2)), dma((2, steps + 1, 2)),
+        dma((2, steps + 1, 2, 2)), dma((2, steps + 1, 2, 2)),
+        dma((2, steps + 1, 2, 2)), dma((2, steps + 1, 2, 2)),
         dma((rows,)), dma((rows,)),
         dma((batch, pairs)), dma((batch, pairs)),
     ]
@@ -742,7 +765,7 @@
             else:
                 ref[0:tpc, cols] = val.astype(BF)
 
-    def group(r, k_s, v_s, scale, pin, p_hbm, start_dq, prefix):
+    def group(r, k_s, v_s, scale, pin, p_hbm, start_dq, prefix, between=None):
         first(r, 0, 0, v_s, scale)
 
         @pl.loop(0, pairs // 2)
@@ -756,56 +779,62 @@
                 @pl.when(i < pairs // 2 - 1)
                 def _():
                     fetch(pin, p_hbm, r, p + 2, u).start()
+            if between is not None:
+                between(r, i)
 
     def to_inputs(at):
         keys = dot(dks[at], w_s[1], NT)
         return keys + dot(dvs[at], w_s[2], NT)
 
     psum[...] = jnp.zeros_like(psum)
-    tails = []
-    y_copies = []
-    b_copies = []
-
-    def chip_sum(r):
-        for copy in b_copies[r]:
-            copy.wait_recv()
-        for d in range(1, chips):
-            y_out[r, d - 1] = (half_b[r, d - 1] + got_b[r, d - 1]).astype(BF)
-        copies = [
-            remote(
-                y_out.at[r, d - 1], y_in.at[r, d - 1], y_send.at[r, d - 1], y_recv.at[r, d - 1], back[d - 1]
-            )
-            for d in range(1, chips)
-        ]
-        for copy in copies:
-            copy.start()
-        y_copies.append(copies)
-
-    for r in range(batch):
+    far = range(1, chips)
+
+    def b_copy(r, d):
+        return remote(
+            send_b.at[r, d - 1], got_b.at[r, d - 1], db_send.at[r, d - 1], db_recv.at[r, d - 1], partner
+        )
+
+    def y_copy(r, d):
+        return remote(
+            y_out.at[r, d - 1], y_in.at[r, d - 1], y_send.at[r, d - 1], y_recv.at[r, d - 1], back[d - 1]
+        )
+
+    def a_copy(r):
+        return remote(send_a.at[r], got_a.at[r], da_send.at[r], da_recv.at[r], partner)
+
+    def out_copy(r):
+        return pltpu.make_async_copy(half_a.at[r], ig_o.at[:, r], o_sem.at[r])
+
+    @pl.loop(0, batch)
+    def _(r):
         group(r, kb, vb, rb, pin_b, pb_i, True, True)
-        if r + 1 < batch:
+
+        @pl.when(r + 1 < batch)
+        def _():
             for u in range(2):
                 fetch(pin_b, pb_i, r + 1, u, u).start()
-        else:
+
+        @pl.when(r + 1 == batch)
+        def _():
             for u in range(2):
                 fetch(pin_a, pa_i, 0, u, u).start()
-        if r == 0:
+
+        @pl.when(r == 0)
+        def _():
             for copy in loads[6:]:
                 copy.wait()
-        copies = []
-        for d in range(1, chips):
+
+        for d in far:
             at = pl.ds(pl.multiple_of((d - 1) * tpc + (1 - core) * per, per), per)
-            send_b[r, d - 1] = to_inputs(at)
-            copy = remote(
-                send_b.at[r, d - 1], got_b.at[r, d - 1], db_send.at[r, d - 1], db_recv.at[r, d - 1], partner
-            )
-            copy.start()
-            copies.append(copy)
-        b_copies.append(copies)
-        for d in range(1, chips):
+            send_b[r, d - 1] = to_inputs(at).astype(BF)
+            b_copy(r, d).start()
+        for d in far:
             at = pl.ds(pl.multiple_of((d - 1) * tpc + core * per, per), per)
-            half_b[r, d - 1] = to_inputs(at)
-        chip_sum(r)
+            half_b[d - 1] = to_inputs(at)
+        for d in far:
+            b_copy(r, d).wait_recv()
+            y_out[r, d - 1] = (half_b[d - 1] + got_b[r, d - 1].astype(F32)).astype(BF)
+            y_copy(r, d).start()
 
     size = 2 * P_SIZE // rows
 
@@ -816,14 +845,78 @@
         remote(psum.at[part(plane[t - 1][0])], pr_in.at[t - 1], p1_send.at[t - 1], p1_recv.at[t - 1], plane[t - 1])
         for t in range(1, rows)
     ]
+    p_two = [remote(pr_y.at[0], pr_y.at[d], p2_send.at[d - 1], p2_recv.at[d - 1], peers[d - 1]) for d in far]
+    p_three = [
+        remote(p_full.at[part(row)], p_full.at[part(row)], p3_send.at[t - 1], p3_recv.at[t - 1], plane[t - 1])
+        for t in range(1, rows)
+    ]
+    cols = pl.ds(col, half)
+    p_four = [
+        remote(
+            p_full.at[k * P_SIZE : (k + 1) * P_SIZE], ref.at[:, cols], p4_send.at[k], p4_recv.at[k], partner
+        )
+        for k, ref in enumerate((pk_o, pv_o))
+    ]
+    p_five = [
+        pltpu.make_async_copy(p_full.at[k * P_SIZE : (k + 1) * P_SIZE], ref.at[:, cols], o_sem.at[batch + k])
+        for k, ref in enumerate((pk_o, pv_o))
+    ]
     for copy in p_one:
         copy.start()
 
-    for r in range(batch):
-        group(r, ka, va, ra, pin_a, pa_i, False, False)
-        if r + 1 < batch:
+    def over_rows():
+        for copy in p_one:
+            copy.wait_recv()
+        total = psum[part(row)]
+        for t in range(1, rows):
+            total = total + pr_in[t - 1]
+        pr_y[0] = total
+        for copy in p_two:
+            copy.start()
+
+    def over_chips():
+        for copy in p_two:
+            copy.wait_recv()
+        whole = jnp.zeros((size, half), F32)
+        for c in range(chips):
+            whole = whole + pr_y[lax.rem(c - chip + chips, chips)]
+        p_full[part(row)] = whole
+        for copy in p_three:
+            copy.start()
+
+    def to_all():
+        for copy in p_three:
+            copy.wait_recv()
+        for copy in p_four + p_five:
+            copy.start()
+
+    def finish(r):
+        a_copy(r).wait_recv()
+        val = half_a[r] + got_a[r].astype(F32)
+        for d in far:
+            y_copy(r, d).wait_recv()
+            val = val + y_in[r, d - 1].astype(F32)
+        half_a[r] = val
+        out_copy(r).start()
+
+    def between(r, i):
+        @pl.when(jnp.logical_and(r == 0, i == 0))
+        def _():
+            over_rows()
+
+        @pl.when(jnp.logical_and(r == 1, i == 0))
+        def _():
+            over_chips()
+
+    @pl.loop(0, batch)
+    def _(r):
+        group(r, ka, va, ra, pin_a, pa_i, False, False, between)
+
+        @pl.when(r + 1 < batch)
+        def _():
             for u in range(2):
                 fetch(pin_a, pa_i, r + 1, u, u).start()
+
         for side in range(2):
             block = pl.multiple_of(((1 - core) if side == 0 else core) * per, per)
             at = pl.ds(block, per)
@@ -832,68 +925,27 @@
                 dvs[at, p * PAIR : (p + 1) * PAIR] = (dq[r, p, at, :]).astype(BF)
             val = part_in + 0.125 * dot(dvs[at], w_s[0], NT)
             if side == 0:
-                send_a[r] = val
-                copy = remote(send_a.at[r], got_a.at[r], da_send.at[r], da_recv.at[r], partner)
-                copy.start()
-                tails.append(copy)
+                send_a[r] = val.astype(BF)
+                a_copy(r).start()
             else:
                 half_a[r] = gs[r] + val
-        if r == 0:
-            for copy in p_one:
-                copy.wait_recv()
-            total = psum[part(row)]
-            for t in range(1, rows):
-                total = total + pr_in[t - 1]
-            pr_y[0] = total
-            p_two = [
-                remote(pr_y.at[0], pr_y.at[d], p2_send.at[d - 1], p2_recv.at[d - 1], peers[d - 1])
-                for d in range(1, chips)
-            ]
-            for copy in p_two:
-                copy.start()
-        if r == batch - 1:
-            for copy in p_two:
-                copy.wait()
-            whole = jnp.zeros((size, half), F32)
-            for c in range(chips):
-                whole = whole + pr_y[lax.rem(c - chip + chips, chips)]
-            p_full[part(row)] = whole
-            p_three = [
-                remote(p_full.at[part(row)], p_full.at[part(row)], p3_send.at[t - 1], p3_recv.at[t - 1], plane[t - 1])
-                for t in range(1, rows)
-            ]
-            for copy in p_three:
-                copy.start()
-
-    outs = []
+
+        @pl.when(r == 1)
+        def _():
+            to_all()
+            finish(0)
+
+    for r in range(1, batch):
+        finish(r)
     for r in range(batch):
-        tails[r].wait()
-        for copy in y_copies[r]:
-            copy.wait()
-        val = half_a[r] + got_a[r]
-        for d in range(1, chips):
-            val = val + y_in[r, d - 1].astype(F32)
-        half_a[r] = val
-        copy = pltpu.make_async_copy(half_a.at[r], ig_o.at[r], o_sem.at[r])
-        copy.start()
-        outs.append(copy)
-    for copy in p_three:
-        copy.wait()
-    cols = pl.ds(col, half)
-    for k, ref in enumerate((pk_o, pv_o)):
-        src = p_full.at[k * P_SIZE : (k + 1) * P_SIZE]
-        copy = remote(src, ref.at[:, cols], p4_send.at[k], p4_recv.at[k], partner)
-        copy.start()
-        outs.append(copy)
-        copy = pltpu.make_async_copy(src, ref.at[:, cols], o_sem.at[batch + k])
-        copy.start()
-        outs.append(copy)
-    for copies in b_copies:
-        for copy in copies:
-            copy.wait_send()
-    for copy in p_one:
+        a_copy(r).wait_send()
+        for d in far:
+            b_copy(r, d).wait_send()
+            y_copy(r, d).wait_send()
+        out_copy(r).wait()
+    for copy in p_one + p_two + p_three:
         copy.wait_send()
-    for copy in outs:
+    for copy in p_four + p_five:
         copy.wait()
 
 
@@ -911,7 +963,7 @@
     return pl.pallas_call(
         functools.partial(backward_kernel, rows, chips),
         out_shape=(
-            out(F32, batch, per, width),
+            out(F32, per, batch, width),
             out(F32, P_SIZE, width),
             out(F32, P_SIZE, width),
         ),
@@ -937,14 +989,11 @@
             vm((keys, half), BF),
             vm((keys, half), BF),
             vm((2 * P_SIZE, half), F32),
-            vm((batch, far, per, width), F32),
-            vm((batch, far, per, width), F32),
-            vm((batch, far, per, width), F32),
-            vm((batch, far, per, width), BF),
-            vm((batch, far, per, width), BF),
+            vm((far, per, width), F32),
+            *([vm((batch, far, per, width), BF)] * 4),
             vm((batch, per, width), F32),
-            vm((batch, per, width), F32),
-            vm((batch, per, width), F32),
+            vm((batch, per, width), BF),
+            vm((batch, per, width), BF),
             vm((rows - 1, size, half), F32),
             vm((chips, size, half), F32),
             vm((2 * P_SIZE, half), F32),
@@ -964,27 +1013,56 @@
     )(g, mix, ra, rb, q, ka, va, kb, vb, pa, pb, wq, wk, wv, gs)
 
 
+def outputs_kernel(pieces, *refs):
+    count = len(refs) // 3
+    srcs, dsts, bufs, sem = refs[:count], refs[count : 2 * count], refs[2 * count : 3 * count], refs[-1]
+    steps = []
+    for k in range(count):
+        size = srcs[k].shape[0] // pieces[k]
+        for i in range(pieces[k]):
+            at = slice(i * size, (i + 1) * size)
+            steps.append(
+                (
+                    pltpu.make_async_copy(srcs[k].at[at], bufs[k].at[at], sem.at[0, k, i]),
+                    pltpu.make_async_copy(bufs[k].at[at], dsts[k].at[at], sem.at[1, k, i]),
+                )
+            )
+    for read, _ in steps:
+        read.start()
+    for read, write in steps:
+        read.wait()
+        write.start()
+    for _, write in steps:
+        write.wait()
+
+
+def outputs_call(*arrays):
+    pieces = [4 if v.ndim == 3 else 1 for v in arrays]
+    return pl.pallas_call(
+        functools.partial(outputs_kernel, pieces),
+        out_shape=tuple(jax.ShapeDtypeStruct(v.shape, v.dtype) for v in arrays),
+        in_specs=[ANY] * len(arrays),
+        out_specs=[ANY] * len(arrays),
+        scratch_shapes=[pltpu.VMEM(v.shape, v.dtype) for v in arrays]
+        + [pltpu.SemaphoreType.DMA((2, len(arrays), 4))],
+        name="outputs",
+    )(*arrays)
+
+
 def on_device(
     rows, chips,
     hidden_in, segments, prefix_vis, prefix_key, prefix_value, w_query, w_key, w_value, w_out,
     norm1_gain, norm1_bias, w_up, w_down, norm2_gain, norm2_bias, out_grad,
 ):
-    x = jnp.transpose(hidden_in, (1, 0, 2))
-    og = jnp.transpose(out_grad, (1, 0, 2))
     flat = lambda v: v.reshape(1, -1)
     q, ka, va, kb, vb, pa, pb, ra, rb, mix, block, gs, g = forward_call(
-        rows, chips, x, segments, prefix_vis, w_query, w_key, w_value, prefix_key, prefix_value,
-        w_out, w_up, w_down, og, flat(norm1_gain), flat(norm1_bias), flat(norm2_gain), flat(norm2_bias),
+        rows, chips, hidden_in, segments, prefix_vis, w_query, w_key, w_value, prefix_key, prefix_value,
+        w_out, w_up, w_down, out_grad, flat(norm1_gain), flat(norm1_bias), flat(norm2_gain), flat(norm2_bias),
     )
     input_grad, pk_grad, pv_grad = backward_call(
         rows, chips, g, mix, ra, rb, q, ka, va, kb, vb, pa, pb, w_query, w_key, w_value, gs
     )
-    return (
-        jnp.transpose(block, (1, 0, 2)),
-        jnp.transpose(input_grad, (1, 0, 2)),
-        pk_grad,
-        pv_grad,
-    )
+    return outputs_call(block, input_grad, pk_grad, pv_grad)
 
 
 def solution(mesh):

time: 152 us -> 139 us (0.914)
  local copies, waits for them, and re-layouts: 13.9 us -> 0 us
    unnamed x12 -> x0, local copies, waits for them, and re-layouts: 13.9 us -> none
    pallas_call x0 -> x1, Pallas kernels: none -> 3.3 us  [outputs_call(): pl.pallas_call(functools.partial(outputs_kernel, pieces), out_shape=tuple...]
    pallas_call x1, Pallas kernels: 90.2 us -> 88.7 us  [forward_call(): pl.pallas_call(functools.partial(forward_kernel, rows, chips), out_shape=...]
where the time goes in v1:
time: 139 us
  Pallas kernels  138 us (99%)
    pallas_call x1, Pallas kernels, forward_call(): pl.pallas_call(functools.partial(forward_kernel, rows, chips), out_shape=...  88.7 us
    pallas_call x1, Pallas kernels, backward_call(): pl.pallas_call(functools.partial(backward_kernel, rows, chips), out_shape...  46.5 us
    pallas_call x1, Pallas kernels, outputs_call(): pl.pallas_call(functools.partial(outputs_kernel, pieces), out_shape=tuple...  3.3 us

profile of v1, /device:TPU:0, one launch (start us, length us, event | category | flops | bytes accessed | tf_op | source)
XLA Modules:
  0.0 139.3 jit_solution(5008685571459740901)
XLA Ops:
  0.6 88.7 %forward_and_ffn.1 = (bf16[2,4,512,128]{3,2,1,0:T(8,128)(2,1)}, bf16[2,4,512,128]{3,2,1,0:T(8,128)(2,1)}, bf16[2,4,512,128]{3,2,1,0:T(8,128)(2,1)}, bf16[2,4,576...) custom-call(bf16[256,2,1024]{2,1,0:T(2,128)(2,1)} %x_own.1, ...), custom_call_target="tpu_custom_call" | custom-call | tf_op jit(solution)/shard_map/forward_and_ffn/pallas_call | solution.py:665
  89.3 46.5 %attention_backward.1 = (f32[256,2,1024]{2,1,0:T(2,128)}, f32[64,1024]{1,0:T(8,128)}, f32[64,1024]{1,0:T(8,128)}) custom-call(bf16[2,4,512,128]{3,2,1,0:T(8,128)(2,1)} %get-tuple-element.21.g_i, bf16[2,4,512,128]{3,2,1,0:T(8,128)(2,1)} %get-tuple-element.22.mix_i, f32[2,4,512,128]{3,2,1,0:T(8,128)} %get-tuple-element.23.ra_i, ...), custom_call_target="tpu_custom_call" | custom-call | tf_op jit(solution)/shard_map/attention_backward/pallas_call | solution.py:963
  135.8 3.3 %outputs.1 = (bf16[256,2,1024]{2,1,0:T(2,128)(2,1)}, f32[256,2,1024]{2,1,0:T(2,128)}, f32[64,1024]{1,0:T(8,128)}, f32[64,1024]{1,0:T(8,128)}) custom-call(bf16[256,2,1024]{2,1,0:T(2,128)(2,1)} %get-tuple-element.20.refs_0_, f32[256,2,1024]{2,1,0:T(2,128)} %get-tuple-element.33.refs_1_, f32[64,1024]{1,0:T(8,128)} %get-tuple-element.34.refs_2_, ...), custom_call_target="tpu_custom_call" | custom-call | tf_op jit(solution)/shard_map/outputs/pallas_call | solution.py:1041

commit v2 on v1

v2 whole, which is shorter than its diff:
```python
import functools

import jax
import jax.numpy as jnp
from jax import lax
from jax.experimental import pallas as pl
from jax.experimental.pallas import tpu as pltpu
from jax.sharding import PartitionSpec as P

E = 64
P_SIZE = 64
SEGS = 4
PAIR = 2 * E
BIG = 1e30
norm_eps = 1e-05
root_half = 0.7071067811865476
inv_root_tau = 0.3989422804014327

BF = jnp.bfloat16
F32 = jnp.float32
MESH = pl.DeviceIdType.MESH
ANY = pl.BlockSpec(memory_space=pl.ANY)
VM = pl.BlockSpec(memory_space=pltpu.VMEM)
NN = (((1,), (0,)), ((), ()))
NT = (((1,), (1,)), ((), ()))
VMEM_LIMIT = 67043328


def dot(a, b, dims=NN):
    return lax.dot_general(a, b, dims, preferred_element_type=F32)


def lanes():
    return lax.broadcasted_iota(jnp.int32, (1, PAIR), 1)


def place():
    row, wide = lax.axis_index("rows"), lax.axis_index("wide")
    return row, wide, lax.rem(wide, 2), lax.div(wide, 2)


def remote(src, dst, send, recv, dev):
    return pltpu.make_async_remote_copy(
        src_ref=src, dst_ref=dst, send_sem=send, recv_sem=recv, device_id=dev, device_id_type=MESH
    )


def ring_pos(row, rows):
    half = rows // 2
    z, x = lax.div(row, 2), lax.rem(row, 2)
    return z + x * (2 * half - 1 - 2 * z)


def ring_row(pos, rows):
    pos = lax.rem(pos + 2 * rows, rows)
    upper = lax.div(pos, rows // 2)
    return 2 * pos + upper * (2 * rows - 1 - 4 * pos)


def mean_of(value):
    return jnp.mean(value, axis=-1, keepdims=True)


def layer_kernel(
    rows, chips,
    x_own, segs, vis, wq, wk, wv, pkey, pval, w_out, w_up, w_dn, og, g1, b1, g2, b2,
    pa_o, pb_o, block_o, ig_o, pk_o, pv_o,
    xbuf, up, dn, wo, mixtok, la, ma, mix_s, g_s, gs, wqkv, q_s, ka, va, kb, vb,
    got_b, y_in, got_a, psum, pr_in, pr_y, p_full, pin_b,
    load_sem, out_sem, p_sem, x_send, x_recv, y_send, y_recv, d_send, d_recv, f_sem, g_sem,
    mx_send, mx_recv, g_send, g_recv, e_send, e_recv, sh_send, sh_recv, r_send, r_recv, k_send, k_recv,
    l_send, l_recv, gm_send, gm_recv,
    db_send, db_recv, yb_send, yb_recv, da_send, da_recv,
    p1_send, p1_recv, p2_send, p2_recv, p3_send, p3_recv, p4_send, p4_recv,
):
    per, batch, width = x_own.shape
    tpc = 2 * per
    rem = (chips - 1) * tpc
    keys_b = rem + P_SIZE
    half = width // 2
    pairs = half // PAIR
    hidden = up.shape[3]
    tokens = batch * per
    row, wide, core, chip = place()
    partner = (row, wide + 1 - 2 * core)
    pos = ring_pos(row, rows)
    nxt = (ring_row(pos + 1, rows), wide)
    prv = (ring_row(pos - 1, rows), wide)
    peers = [(row, 2 * lax.rem(chip - d + chips, chips) + core) for d in range(1, chips)]
    mats = ((w_up, up), (w_dn, dn))
    cw = (rows // 2, 3)
    ccw = (rows // 2 - 1, 3)
    cuts = (1, 1)
    plane = [(lax.rem(row + t, rows), wide) for t in range(1, rows)]
    back = [(row, 2 * lax.rem(chip + d, chips) + core) for d in range(1, chips)]

    col = pl.multiple_of(core * half, half)
    far_loads = [
        pltpu.make_async_copy(w_up, up.at[0, core], load_sem.at[0]),
        pltpu.make_async_copy(w_dn, dn.at[0, core], load_sem.at[1]),
        pltpu.make_async_copy(w_out, wo, load_sem.at[2]),
    ]

    x_pair = remote(xbuf.at[:, 0, core], xbuf.at[:, 0, core], x_send, x_recv, partner)
    cross = [
        [
            remote(xbuf.at[r, 0, core], xbuf.at[r, d, core], y_send.at[r, d - 1], y_recv.at[r, d - 1], peers[d - 1])
            for d in range(1, chips)
        ]
        for r in range(batch)
    ]

    def piece(ref, row_at, cut=0, cuts_of=1):
        size = ref.shape[-2] // rows
        sub = size // cuts_of
        return pl.ds(pl.multiple_of(row_at * size + cut * sub, sub), sub)

    def w_cross(m, row_at, cut, cuts_of, send, recv):
        src, dst = mats[m]
        at = piece(src, row_at, cut, cuts_of)
        return [
            remote(src.at[at], dst.at[d, core, at], send.at[d - 1], recv.at[d - 1], peers[d - 1])
            for d in range(1, chips)
        ]

    split_cross = [
        [w_cross(m, row, h, cuts[m], g_send.at[m, h], g_recv.at[m, h]) for h in range(cuts[m])] for m in range(2)
    ]
    wcross = [sum(group, []) for group in split_cross]
    far_off = range(ccw[1] + 1, rows - cw[1])
    extras = sum([w_cross(1, ring_row(pos + o, rows), 0, 1, e_send.at[o], e_recv.at[o]) for o in far_off], [])
    shards = [
        remote(mats[m][0], mats[m][1].at[0, core], sh_send.at[m], sh_recv.at[m], partner) for m in range(2)
    ]

    def place_of(s, way):
        return ring_row(pos - s if way == 0 else pos + s, rows)

    def ring_copy(m, s, way, h):
        buf = mats[m][1]
        ref = buf.at[1:, core, piece(buf, place_of(s - 1, way), h, cuts[m])]
        return remote(ref, ref, r_send.at[m, s, way, h], r_recv.at[m, s, way, h], nxt if way == 0 else prv)

    def hand_over(m, s, way, h):
        buf = mats[m][1]
        ref = buf.at[1:, core, piece(buf, place_of(s, way), h, cuts[m])]
        return remote(ref, ref, k_send.at[m, s, way, h], k_recv.at[m, s, way, h], partner)

    def ways(m, s):
        return range(2 if s <= ccw[m] else 1)

    def hop(m, s, h=0):
        if s > cw[m] + 1 or h >= cuts[m]:
            return
        if s == 1:
            for copy in split_cross[m][h]:
                copy.wait_recv()
        else:
            for way in ways(m, s - 1):
                ring_copy(m, s - 1, way, h).wait_recv()
        if s <= cw[m]:
            for way in ways(m, s):
                ring_copy(m, s, way, h).start()
        for way in ways(m, s - 1) if s > 1 else range(1):
            hand_over(m, s - 1, way, h).start()

    def extra_over(o):
        buf = mats[1][1]
        ref = buf.at[1:, core, piece(buf, place_of(o, 1))]
        return remote(ref, ref, l_send.at[o], l_recv.at[o], partner)

    def take_extras():
        for copy in extras:
            copy.wait_recv()
        for o in far_off:
            extra_over(o).start()

    def all_over(m):
        copies = [hand_over(m, 0, 0, h) for h in range(cuts[m])]
        for s in range(1, cw[m] + 1):
            copies += [hand_over(m, s, way, h) for way in ways(m, s) for h in range(cuts[m])]
        if m == 1:
            copies += [extra_over(o) for o in far_off]
        return copies

    def gathered(m):
        for copy in all_over(m):
            copy.wait_recv()

    def sent(m):
        for copy in wcross[m] + all_over(m) + (extras if m == 1 else []):
            copy.wait_send()
        for s in range(1, cw[m] + 1):
            for way in ways(m, s):
                for h in range(cuts[m]):
                    ring_copy(m, s, way, h).wait_send()

    mine_at, other_at = pl.multiple_of(core * per, per), pl.multiple_of((1 - core) * per, per)

    def mix_out(r, p):
        cols = pl.ds(pl.multiple_of(core * half + p * PAIR, PAIR), PAIR)
        dst = mixtok.at[pl.ds(pl.multiple_of(r * per, per), per), cols]
        return (
            remote(mix_s.at[r, p, pl.ds(other_at, per)], dst, mx_send.at[r, p], mx_recv.at[r, p], partner),
            pltpu.make_async_copy(mix_s.at[r, p, pl.ds(mine_at, per)], dst, f_sem.at[r, p]),
        )

    def attention(pks, pvs, s0, s1, s2, s3, oa, pst_a, pst_b, qe, kea, keb, xraw):
        x_load = pltpu.make_async_copy(x_own, xraw, load_sem.at[3 + batch])
        loads = [
            pltpu.make_async_copy(wq.at[:, pl.ds(col, half)], wqkv.at[:, 0:half], load_sem.at[4 + batch]),
            pltpu.make_async_copy(wk.at[:, pl.ds(col, half)], wqkv.at[:, half : 2 * half], load_sem.at[5 + batch]),
            pltpu.make_async_copy(wv.at[:, pl.ds(col, half)], wqkv.at[:, 2 * half : 3 * half], load_sem.at[6 + batch]),
            pltpu.make_async_copy(pkey.at[:, pl.ds(col, half)], pks, load_sem.at[7 + batch]),
            pltpu.make_async_copy(pval.at[:, pl.ds(col, half)], pvs, load_sem.at[8 + batch]),
        ]
        barrier = pltpu.get_barrier_semaphore()
        friends = [partner] + plane + peers
        for dev in friends:
            pl.semaphore_signal(barrier, inc=1, device_id=dev, device_id_type=MESH)
        x_load.start()
        for copy in loads:
            copy.start()
        x_load.wait()
        for r in range(batch):
            xbuf[r, 0, core] = xraw[:, r, :]
        pl.semaphore_wait(barrier, len(friends))
        x_pair.start()
        for group in wcross + cross + [extras]:
            for copy in group:
                copy.start()
        for copy in shards + far_loads:
            copy.start()

        term = lax.broadcasted_iota(jnp.int32, (PAIR, 1), 0)
        term = jnp.where(term >= E, term - E, term)

        def key_terms(seg):
            off = jnp.where(jnp.logical_and(term < SEGS, seg != term), -BIG, 0.0)
            return off.T.astype(BF)

        for r in range(batch):
            for d in range(chips):
                at = pl.multiple_of(lax.rem(chip + d, chips) * tpc, tpc)
                seg = segs[r : r + 1, pl.ds(at, tpc)]
                if d == 0:
                    kea[r] = key_terms(seg)
                    on = jnp.logical_or(term == SEGS, jnp.logical_and(term < SEGS, seg == term))
                    qe[r] = jnp.where(on, 1.0, 0.0).T.astype(BF)
                else:
                    keb[r, (d - 1) * tpc : d * tpc] = key_terms(seg)
            unseen = jnp.logical_and(term == SEGS, vis[r : r + 1, :] == 0)
            keb[r, rem:] = jnp.where(unseen, -BIG, 0.0).T.astype(BF)

        def project(r, d, cb, with_q):
            x = xbuf[r, d, cb]
            if with_q:
                q = (dot(x, wqkv[:, 0:half]) * 0.125).astype(BF)
                for p in range(pairs):
                    q_s[r, p, pl.ds(pl.multiple_of(cb * per, per), per), :] = q[:, p * PAIR : (p + 1) * PAIR]
            for ref_a, ref_b, at in ((ka, kb, 1), (va, vb, 2)):
                y = dot(x, wqkv[:, at * half : (at + 1) * half]).astype(BF)
                for p in range(pairs):
                    val = y[:, p * PAIR : (p + 1) * PAIR]
                    if with_q:
                        ref_a[r, p, pl.ds(pl.multiple_of(cb * per, per), per), :] = val
                    else:
                        ref_b[r, p, pl.ds(pl.multiple_of((d - 1) * tpc + cb * per, per), per), :] = val

        for copy in loads:
            copy.wait()
        for r in range(batch):
            for p in range(pairs):
                kb[r, p, rem:, :] = pks[:, p * PAIR : (p + 1) * PAIR]
                vb[r, p, rem:, :] = pvs[:, p * PAIR : (p + 1) * PAIR]

        @pl.loop(0, 2 * batch)
        def _(i):
            pl.when(i == batch)(x_pair.wait_recv)
            late = lax.div(i, batch)
            project(lax.rem(i, batch), 0, core + late - 2 * core * late, True)

        hop(0, 1)
        bufs = (s0, s1, s2, s3)

        def score(r, p, h, k_s, kext, buf):
            keys = k_s.shape[2]
            mine = lanes() < E if h == 0 else lanes() >= E
            q = jnp.where(mine, q_s[r, p], qe[r])
            k = jnp.where(mine, k_s[r, p], kext[r])
            buf[:, 0:keys] = dot(q, k, NT)

        def unit(r, p, after, u, k_s, v_s, kext, pst, p_hbm, finish, wait_slot):
            keys = k_s.shape[2]
            copy = pltpu.make_async_copy(pst.at[u], p_hbm.at[r, p], p_sem.at[u])
            pl.when(wait_slot)(copy.wait)
            tops, sums = [], []
            for h in range(2):
                score(after[0], after[1], h, k_s, kext, bufs[2 * (1 - u) + h])
                s = bufs[2 * u + h][:, 0:keys]
                top = jnp.max(s, axis=1, keepdims=True)
                prob = jnp.exp(s - top).astype(BF)
                pst[u, h] = prob
                mine = lanes() < E if h == 0 else lanes() >= E
                v = jnp.where(mine, v_s[r, p], jnp.ones((1, PAIR), BF))
                sums.append(dot(prob, v))
                tops.append(top)
            copy.start()
            low = lanes() < E
            finish(
                r,
                p,
                jnp.where(low, sums[0], sums[1]),
                pltpu.roll(jnp.where(low, sums[1], sums[0]), E, 1),
                jnp.where(low, tops[0], tops[1]),
            )

        def finish_a(r, p, o, l, m):
            oa[r, p], la[r, p], ma[r, p] = o, l, m

        def finish_b(r, p, o, l, m):
            top = jnp.maximum(ma[r, p], m)
            w_a, w_b = jnp.exp(ma[r, p] - top), jnp.exp(m - top)
            inv = 1.0 / (w_a * la[r, p] + w_b * l)
            r_a, r_b = w_a * inv, w_b * inv
            mix_s[r, p] = (oa[r, p] * r_a + o * r_b).astype(BF)
            la[r, p], ma[r, p] = r_a, r_b

        def drain(pst, p_hbm):
            for u in range(2):
                pltpu.make_async_copy(pst.at[u], p_hbm.at[0, 0], p_sem.at[u]).wait()

        args_a = (ka, va, kea, pst_a, pa_o, finish_a)
        for h in range(2):
            score(0, 0, h, ka, kea, bufs[h])
        count = batch * pairs

        @pl.loop(0, count // 2)
        def _(i):
            for u in range(2):
                j = 2 * i + u
                after = jnp.minimum(j + 1, count - 1)
                unit(
                    lax.div(j, pairs), lax.rem(j, pairs), (lax.div(after, pairs), lax.rem(after, pairs)),
                    u, *args_a, i > 0,
                )

            @pl.when(i == 2)
            def _():
                hop(1, 1)

        drain(pst_a, pa_o)
        hop(0, 2)
        hop(1, 2)

        args_b = (kb, vb, keb, pst_b, pb_o, finish_b)

        @pl.loop(0, batch)
        def _(r):
            for d in range(1, chips):
                remote(
                    xbuf.at[r, 0, core], xbuf.at[r, d, core], y_send.at[r, d - 1], y_recv.at[r, d - 1], peers[d - 1]
                ).wait_recv()
            forward = remote(
                xbuf.at[r, 1:, core], xbuf.at[r, 1:, core], d_send.at[r], d_recv.at[r], partner
            )
            forward.start()

            @pl.loop(0, 2 * (chips - 1))
            def _(i):
                pl.when(i == chips - 1)(forward.wait_recv)
                late = lax.div(i, chips - 1)
                project(r, lax.rem(i, chips - 1) + 1, core + late - 2 * core * late, False)

            @pl.when(r == 0)
            def _():
                hop(0, 3)

            @pl.when(r == 1)
            def _():
                hop(0, 4)

            for h in range(2):
                score(r, 0, h, kb, keb, bufs[h])

            @pl.loop(0, pairs // 2)
            def _(i):
                for u in range(2):
                    p = 2 * i + u
                    unit(r, p, (r, jnp.minimum(p + 1, pairs - 1)), u, *args_b, i > 0)

            drain(pst_b, pb_o)
            for p in range(pairs):
                for copy in mix_out(r, p):
                    copy.start()
            forward.wait_send()

            @pl.when(r == 0)
            def _():
                hop(1, 3)

        for s in range(5, cw[0] + 1):
            hop(0, s)
        hop(1, 4)
        take_extras()
        x_pair.wait_send()

    vm = pltpu.VMEM
    keys = max(tpc, keys_b)
    pl.run_scoped(
        attention,
        vm((P_SIZE, half), BF),
        vm((P_SIZE, half), BF),
        *([vm((tpc, keys), F32)] * 4),
        vm((batch, pairs, tpc, PAIR), F32),
        vm((2, 2, tpc, tpc), BF),
        vm((2, 2, tpc, keys_b), BF),
        vm((batch, tpc, PAIR), BF),
        vm((batch, tpc, PAIR), BF),
        vm((batch, keys_b, PAIR), BF),
        vm((per, batch, width), BF),
    )

    tile = min(512, hidden)
    tiles = hidden // tile
    total = 2 * chips * tiles
    chunk = 64

    def fetch(pin, p_hbm, r, p, u):
        return pltpu.make_async_copy(p_hbm.at[r, p], pin.at[u], p_sem.at[u])

    def feed_forward(ogs, gst, sc1, inv1, acc, slope, pre0, pre1, bst):
        nl = mixtok
        og_loads = [pltpu.make_async_copy(og.at[:, r], ogs.at[r], load_sem.at[3 + r]) for r in range(batch)]
        for copy in og_loads:
            copy.start()
        for u in range(2):
            fetch(pin_b, pb_o, 0, u, u).start()
        for copy in far_loads:
            copy.wait()
        for r in range(batch):
            for p in range(pairs):
                for copy in mix_out(r, p):
                    copy.wait()

        @pl.loop(0, width // 256)
        def _(j):
            at = pl.ds(pl.multiple_of(j * 256, 256), 256)
            acc[:, at] = dot(mixtok[...], wo[:, at])

        def by_rows(body):
            for r in range(batch):

                @pl.loop(0, per // chunk, unroll=min(2, per // chunk))
                def _(i, r=r):
                    inner = pl.ds(pl.multiple_of(i * chunk, chunk), chunk)
                    body(r, inner, pl.ds(pl.multiple_of(r * per + i * chunk, chunk), chunk))

        def norm_one(r, inner, at):
            z = acc[at] + xbuf[r, 0, core, inner].astype(F32)
            c = z - mean_of(z)
            inv = lax.rsqrt(mean_of(c * c) + norm_eps)
            s = c * inv
            n = s * g1[...] + b1[...]
            nl[at], sc1[at], inv1[at] = n.astype(BF), s, inv
            acc[at] = jnp.zeros_like(z)

        by_rows(norm_one)
        for copy in shards + og_loads:
            copy.wait()

        def split(j):
            slot = lax.div(j, tiles)
            at = pl.ds(pl.multiple_of(lax.rem(j, tiles) * tile, tile), tile)
            return lax.div(slot, 2), lax.rem(slot, 2), at

        def up_tile(j, buf):
            d, c, at = split(j)
            buf[...] = dot(nl[...], up[d, c, :, at])

        pres = (pre0, pre1)
        up_tile(0, pre0)

        @pl.loop(0, total // 2)
        def _(i):
            @pl.when(i == max(tiles - 1, 0))
            def _():
                hop(0, cw[0] + 1)
                gathered(0)

            @pl.when(i == tiles)
            def _():
                gathered(1)

            for u in range(2):
                j = 2 * i + u
                up_tile(jnp.minimum(j + 1, total - 1), pres[1 - u])
                v = pres[u][...]
                cdf = 0.5 * (1.0 + lax.erf(v * root_half))
                a = (v * cdf).astype(BF)
                d, c, at = split(j)
                slope[j] = (cdf + v * jnp.exp(-0.5 * v * v) * inv_root_tau).astype(BF)
                acc[...] += dot(a, dn[d, c, at, :])

        def norm_two(r, inner, at):
            z = sc1[at] * g1[...] + b1[...] + acc[at]
            c = z - mean_of(z)
            inv = lax.rsqrt(mean_of(c * c) + norm_eps)
            s = c * inv
            bst[inner, r, :] = (s * g2[...] + b2[...]).astype(BF)
            t = ogs[r, inner] * g2[...]
            g = inv * (t - mean_of(t) - s * mean_of(t * s))
            gs[at], nl[at] = g, g.astype(BF)
            acc[at] = jnp.zeros_like(z)

        by_rows(norm_two)
        outs = [pltpu.make_async_copy(bst, block_o, out_sem.at[0])]
        outs[0].start()

        def down_back(j, buf):
            d, c, at = split(j)
            buf[...] = dot(nl[...], dn[d, c, at, :], NT)

        down_back(0, pre0)

        @pl.loop(0, total // 2)
        def _(i):
            for u in range(2):
                j = 2 * i + u
                down_back(jnp.minimum(j + 1, total - 1), pres[1 - u])
                g = (pres[u][...] * slope[j].astype(F32)).astype(BF)
                d, c, at = split(j)
                acc[...] += dot(g, up[d, c, :, at], NT)

        def norm_back(r, inner, at):
            t = (gs[at] + acc[at]) * g1[...]
            s = sc1[at]
            g = inv1[at] * (t - mean_of(t) - s * mean_of(t * s))
            gs[at], nl[at] = g, g.astype(BF)

        by_rows(norm_back)
        mine = pl.ds(mine_at, per)
        for side in range(2):
            base = (1 - core) * half if side == 0 else core * half
            g = dot(nl[...], wo[pl.ds(pl.multiple_of(base, half), half), :], NT).astype(BF)
            for p in range(pairs):
                for r in range(batch):
                    val = g[r * per : (r + 1) * per, p * PAIR : (p + 1) * PAIR]
                    if side == 0:
                        gst[r, p] = val
                    else:
                        g_s[r, p, mine, :] = val
            if side == 0:
                sends = [
                    remote(gst.at[r, p], g_s.at[r, p, mine], gm_send.at[r, p], gm_recv.at[r, p], partner)
                    for r in range(batch)
                    for p in range(pairs)
                ]
                for copy in sends:
                    copy.start()
        for copy in sends + outs:
            copy.wait()

    pl.run_scoped(
        feed_forward,
        vm((batch, per, width), F32),
        vm((batch, pairs, per, PAIR), BF),
        vm((tokens, width), F32),
        vm((tokens, 1), F32),
        vm((tokens, width), F32),
        vm((total, tokens, tile), BF),
        vm((tokens, tile), F32),
        vm((tokens, tile), F32),
        vm((per, batch, width), BF),
    )

    def attention_back(pin_a, s0, s1, s2, s3, do0, do1, dq, dks, dvs, half_b, send_b, y_out, send_a):
        bufs, dos = (s0, s1, s2, s3), (do0, do1)

        def first(r, p, u, v_s, scale):
            keys = v_s.shape[2]
            g = g_s[r, p].astype(F32) * scale[r, p]
            do = g.astype(BF)
            dos[u][...] = do
            t = g * mix_s[r, p].astype(F32)
            lane = lanes()
            for h in range(2):
                mine = lane < E if h == 0 else lane >= E
                delta = jnp.sum(jnp.where(mine, t, 0.0), axis=1, keepdims=True)
                hi = delta.astype(BF)
                left = delta - hi.astype(F32)
                mid = left.astype(BF)
                low = (left - mid.astype(F32)).astype(BF)
                at = E if h == 0 else 0
                ext = jnp.where(
                    lane == at, -hi, jnp.where(lane == at + 1, -mid, jnp.where(lane == at + 2, -low, jnp.zeros((1, PAIR), BF)))
                )
                one = jnp.where(jnp.logical_and(lane >= at, lane < at + 3), 1.0, 0.0).astype(BF)
                bufs[2 * u + h][:, 0:keys] = dot(
                    jnp.where(mine, do, ext), jnp.where(mine, v_s[r, p], one), NT
                )

        def second(r, p, u, k_s, pin, start_dq, prefix):
            keys = k_s.shape[2]
            q2, k2, do = q_s[r, p], k_s[r, p], dos[u][...]
            do_t, q_t = do.T, q2.T
            gq, gk, gv = [], [], []
            for h in range(2):
                prob = pin[u, h]
                ds = (prob.astype(F32) * bufs[2 * u + h][:, 0:keys]).astype(BF)
                at = slice(h * E, (h + 1) * E)
                gv.append(dot(do_t[at], prob))
                gk.append(dot(q_t[at], ds))
                gq.append(dot(ds, k2))
            low = lanes() < E
            grad = jnp.where(low, gq[0], gq[1])
            dq[r, p] = grad if start_dq else dq[r, p] + grad
            cols = pl.ds(pl.multiple_of(p * PAIR, PAIR), PAIR)
            for ref, parts, k in ((dks, gk, 0), (dvs, gv, 1)):
                val = jnp.concatenate(parts, axis=0).T
                if prefix:
                    ref[0:rem, cols] = val[:rem].astype(BF)
                    psum[k * P_SIZE : (k + 1) * P_SIZE, cols] += val[rem:]
                else:
                    ref[0:tpc, cols] = val.astype(BF)

        def group(r, k_s, v_s, scale, pin, p_hbm, start_dq, prefix, between=None):
            first(r, 0, 0, v_s, scale)

            @pl.loop(0, pairs // 2)
            def _(i):
                for u in range(2):
                    p = 2 * i + u
                    fetch(pin, p_hbm, r, p, u).wait()
                    first(r, jnp.minimum(p + 1, pairs - 1), 1 - u, v_s, scale)
                    second(r, p, u, k_s, pin, start_dq, prefix)

                    @pl.when(i < pairs // 2 - 1)
                    def _():
                        fetch(pin, p_hbm, r, p + 2, u).start()
                if between is not None:
                    between(r, i)

        def to_inputs(at):
            keys = dot(dks[at], wqkv[:, half : 2 * half], NT)
            return keys + dot(dvs[at], wqkv[:, 2 * half : 3 * half], NT)

        psum[...] = jnp.zeros_like(psum)
        far = range(1, chips)

        def b_copy(r, d):
            return remote(
                send_b.at[r, d - 1], got_b.at[r, d - 1], db_send.at[r, d - 1], db_recv.at[r, d - 1], partner
            )

        def y_copy(r, d):
            return remote(
                y_out.at[r, d - 1], y_in.at[r, d - 1], yb_send.at[r, d - 1], yb_recv.at[r, d - 1], back[d - 1]
            )

        def a_copy(r):
            return remote(send_a.at[r], got_a.at[r], da_send.at[r], da_recv.at[r], partner)

        def token_rows(r):
            return pl.ds(pl.multiple_of(r * per, per), per)

        def out_copy(r):
            return pltpu.make_async_copy(gs.at[token_rows(r)], ig_o.at[:, r], out_sem.at[r])

        @pl.loop(0, batch)
        def _(r):
            group(r, kb, vb, ma, pin_b, pb_o, True, True)

            @pl.when(r + 1 < batch)
            def _():
                for u in range(2):
                    fetch(pin_b, pb_o, r + 1, u, u).start()

            @pl.when(r + 1 == batch)
            def _():
                for u in range(2):
                    fetch(pin_a, pa_o, 0, u, u).start()

            for d in far:
                at = pl.ds(pl.multiple_of((d - 1) * tpc + (1 - core) * per, per), per)
                send_b[r, d - 1] = to_inputs(at).astype(BF)
                b_copy(r, d).start()
            for d in far:
                at = pl.ds(pl.multiple_of((d - 1) * tpc + core * per, per), per)
                half_b[d - 1] = to_inputs(at)
            for d in far:
                b_copy(r, d).wait_recv()
                y_out[r, d - 1] = (half_b[d - 1] + got_b[r, d - 1].astype(F32)).astype(BF)
                y_copy(r, d).start()

        size = 2 * P_SIZE // rows

        def part(at):
            return pl.ds(pl.multiple_of(at * size, size), size)

        p_one = [
            remote(psum.at[part(plane[t - 1][0])], pr_in.at[t - 1], p1_send.at[t - 1], p1_recv.at[t - 1], plane[t - 1])
            for t in range(1, rows)
        ]
        p_two = [remote(pr_y.at[0], pr_y.at[d], p2_send.at[d - 1], p2_recv.at[d - 1], peers[d - 1]) for d in far]
        p_three = [
            remote(p_full.at[part(row)], p_full.at[part(row)], p3_send.at[t - 1], p3_recv.at[t - 1], plane[t - 1])
            for t in range(1, rows)
        ]
        cols = pl.ds(col, half)
        p_four = [
            remote(
                p_full.at[k * P_SIZE : (k + 1) * P_SIZE], ref.at[:, cols], p4_send.at[k], p4_recv.at[k], partner
            )
            for k, ref in enumerate((pk_o, pv_o))
        ]
        p_five = [
            pltpu.make_async_copy(p_full.at[k * P_SIZE : (k + 1) * P_SIZE], ref.at[:, cols], out_sem.at[batch + k])
            for k, ref in enumerate((pk_o, pv_o))
        ]
        for copy in p_one:
            copy.start()

        def over_rows():
            for copy in p_one:
                copy.wait_recv()
            total = psum[part(row)]
            for t in range(1, rows):
                total = total + pr_in[t - 1]
            pr_y[0] = total
            for copy in p_two:
                copy.start()

        def over_chips():
            for copy in p_two:
                copy.wait_recv()
            whole = jnp.zeros((size, half), F32)
            for c in range(chips):
                whole = whole + pr_y[lax.rem(c - chip + chips, chips)]
            p_full[part(row)] = whole
            for copy in p_three:
                copy.start()

        def to_all():
            for copy in p_three:
                copy.wait_recv()
            for copy in p_four + p_five:
                copy.start()

        def finish(r):
            a_copy(r).wait_recv()
            val = gs[token_rows(r)] + got_a[r].astype(F32)
            for d in far:
                y_copy(r, d).wait_recv()
                val = val + y_in[r, d - 1].astype(F32)
            gs[token_rows(r)] = val
            out_copy(r).start()

        def between(r, i):
            @pl.when(jnp.logical_and(r == 0, i == 0))
            def _():
                over_rows()

            @pl.when(jnp.logical_and(r == 1, i == 0))
            def _():
                over_chips()

        @pl.loop(0, batch)
        def _(r):
            group(r, ka, va, la, pin_a, pa_o, False, False, between)

            @pl.when(r + 1 < batch)
            def _():
                for u in range(2):
                    fetch(pin_a, pa_o, r + 1, u, u).start()

            for side in range(2):
                block = pl.multiple_of(((1 - core) if side == 0 else core) * per, per)
                at = pl.ds(block, per)
                part_in = to_inputs(at)
                for p in range(pairs):
                    dvs[at, p * PAIR : (p + 1) * PAIR] = (dq[r, p, at, :]).astype(BF)
                val = part_in + 0.125 * dot(dvs[at], wqkv[:, 0:half], NT)
                if side == 0:
                    send_a[r] = val.astype(BF)
                    a_copy(r).start()
                else:
                    gs[token_rows(r)] += val

            @pl.when(r == 1)
            def _():
                to_all()
                finish(0)

        for r in range(1, batch):
            finish(r)
        for r in range(batch):
            a_copy(r).wait_send()
            for d in far:
                b_copy(r, d).wait_send()
                y_copy(r, d).wait_send()
            out_copy(r).wait()
        for copy in p_one + p_two + p_three:
            copy.wait_send()
        for copy in p_four + p_five:
            copy.wait()

    pl.run_scoped(
        attention_back,
        vm((2, 2, tpc, tpc), BF),
        *([vm((tpc, keys), F32)] * 4),
        *([vm((tpc, PAIR), BF)] * 2),
        vm((batch, pairs, tpc, PAIR), F32),
        vm((keys, half), BF),
        vm((keys, half), BF),
        vm((chips - 1, per, width), F32),
        *([vm((batch, chips - 1, per, width), BF)] * 2),
        vm((batch, per, width), BF),
    )
    for r in range(batch):
        for copy in cross[r]:
            copy.wait_send()
    for m in range(2):
        sent(m)


def layer_call(rows, chips, x, segs, vis, wq, wk, wv, pkey, pval, w_out, w_up, w_dn, og, g1, b1, g2, b2):
    per, batch, width = x.shape
    tpc, half = 2 * per, width // 2
    far = chips - 1
    keys_b = far * tpc + P_SIZE
    pairs = half // PAIR
    tokens = batch * per
    steps = rows // 2
    size = 2 * P_SIZE // rows
    out = lambda dt, *s: jax.ShapeDtypeStruct(s, dt)
    shapes = (
        out(BF, batch, pairs, 2, tpc, tpc),
        out(BF, batch, pairs, 2, tpc, keys_b),
        out(BF, per, batch, width),
        out(F32, per, batch, width),
        out(F32, P_SIZE, width),
        out(F32, P_SIZE, width),
    )
    dma = pltpu.SemaphoreType.DMA
    vm = pltpu.VMEM
    scratch = [
        vm((batch, chips, 2, per, width), BF),
        vm((chips, 2, *w_up.shape), BF),
        vm((chips, 2, *w_dn.shape), BF),
        vm((width, width), BF),
        vm((tokens, width), BF),
        vm((batch, pairs, tpc, PAIR), F32),
        vm((batch, pairs, tpc, PAIR), F32),
        vm((batch, pairs, tpc, PAIR), BF),
        vm((batch, pairs, tpc, PAIR), BF),
        vm((tokens, width), F32),
        vm((width, 3 * half), BF),
        vm((batch, pairs, tpc, PAIR), BF),
        vm((batch, pairs, tpc, PAIR), BF),
        vm((batch, pairs, tpc, PAIR), BF),
        vm((batch, pairs, keys_b, PAIR), BF),
        vm((batch, pairs, keys_b, PAIR), BF),
        vm((batch, far, per, width), BF),
        vm((batch, far, per, width), BF),
        vm((batch, per, width), BF),
        vm((2 * P_SIZE, half), F32),
        vm((rows - 1, size, half), F32),
        vm((chips, size, half), F32),
        vm((2 * P_SIZE, half), F32),
        vm((2, 2, tpc, keys_b), BF),
        dma((9 + batch,)), dma((5,)), dma((2,)), dma, dma,
        dma((batch, far)), dma((batch, far)),
        dma((batch,)), dma((batch,)),
        dma((batch, pairs)), dma((batch, pairs)),
        dma((batch, pairs)), dma((batch, pairs)),
        dma((2, 2, far)), dma((2, 2, far)),
        dma((rows, far)), dma((rows, far)),
        dma((2,)), dma((2,)),
        dma((2, steps + 1, 2, 2)), dma((2, steps + 1, 2, 2)),
        dma((2, steps + 1, 2, 2)), dma((2, steps + 1, 2, 2)),
        dma((rows,)), dma((rows,)),
        dma((batch, pairs)), dma((batch, pairs)),
        dma((batch, far)), dma((batch, far)),
        dma((batch, far)), dma((batch, far)),
        dma((batch,)), dma((batch,)),
        dma((rows - 1,)), dma((rows - 1,)),
        dma((far,)), dma((far,)),
        dma((rows - 1,)), dma((rows - 1,)),
        dma((2,)), dma((2,)),
    ]
    return pl.pallas_call(
        functools.partial(layer_kernel, rows, chips),
        out_shape=shapes,
        in_specs=[ANY] + [VM] * 2 + [ANY] * 9 + [VM] * 4,
        out_specs=[ANY] * len(shapes),
        scratch_shapes=scratch,
        compiler_params=pltpu.CompilerParams(
            collective_id=0, has_side_effects=True, vmem_limit_bytes=VMEM_LIMIT
        ),
        name="layer",
    )(x, segs, vis, wq, wk, wv, pkey, pval, w_out, w_up, w_dn, og, g1, b1, g2, b2)


def outputs_kernel(pieces, *refs):
    count = len(refs) // 3
    srcs, dsts, bufs, sem = refs[:count], refs[count : 2 * count], refs[2 * count : 3 * count], refs[-1]
    steps = []
    for k in range(count):
        size = srcs[k].shape[0] // pieces[k]
        for i in range(pieces[k]):
            at = slice(i * size, (i + 1) * size)
            steps.append(
                (
                    pltpu.make_async_copy(srcs[k].at[at], bufs[k].at[at], sem.at[0, k, i]),
                    pltpu.make_async_copy(bufs[k].at[at], dsts[k].at[at], sem.at[1, k, i]),
                )
            )
    for read, _ in steps:
        read.start()
    for read, write in steps:
        read.wait()
        write.start()
    for _, write in steps:
        write.wait()


def outputs_call(*arrays):
    pieces = [4 if v.ndim == 3 else 1 for v in arrays]
    return pl.pallas_call(
        functools.partial(outputs_kernel, pieces),
        out_shape=tuple(jax.ShapeDtypeStruct(v.shape, v.dtype) for v in arrays),
        in_specs=[ANY] * len(arrays),
        out_specs=[ANY] * len(arrays),
        scratch_shapes=[pltpu.VMEM(v.shape, v.dtype) for v in arrays]
        + [pltpu.SemaphoreType.DMA((2, len(arrays), 4))],
        name="outputs",
    )(*arrays)


def on_device(
    rows, chips,
    hidden_in, segments, prefix_vis, prefix_key, prefix_value, w_query, w_key, w_value, w_out,
    norm1_gain, norm1_bias, w_up, w_down, norm2_gain, norm2_bias, out_grad,
):
    flat = lambda v: v.reshape(1, -1)
    _, _, block, input_grad, pk_grad, pv_grad = layer_call(
        rows, chips, hidden_in, segments, prefix_vis, w_query, w_key, w_value, prefix_key, prefix_value,
        w_out, w_up, w_down, out_grad, flat(norm1_gain), flat(norm1_bias), flat(norm2_gain), flat(norm2_bias),
    )
    return outputs_call(block, input_grad, pk_grad, pv_grad)


def solution(mesh):
    rows, chips = mesh.shape["rows"], mesh.shape["wide"] // 2
    act = P("wide", "rows", None)
    per_row = P("rows", None)
    in_specs = (
        act, per_row, per_row, *([P()] * 8), P(None, "wide"), P("wide", None), P(), P(), act,
    )
    out_specs = (act, act, P(), P())
    return jax.shard_map(
        functools.partial(on_device, rows, chips),
        mesh=mesh,
        in_specs=in_specs,
        out_specs=out_specs,
        check_vma=False,
    )
```

time: 139 us -> 134 us (0.964)
  Pallas kernels: 138 us -> 133 us
    pallas_call x2 -> x1, Pallas kernels: 135 us -> 130 us  [layer_call(): pl.pallas_call(functools.partial(layer_kernel, rows, chips), out_shape=sh...]
where the time goes in v2:
time: 134 us
  Pallas kernels  133 us (99%)
    pallas_call x1, Pallas kernels, layer_call(): pl.pallas_call(functools.partial(layer_kernel, rows, chips), out_shape=sh...  130 us
    pallas_call x1, Pallas kernels, outputs_call(): pl.pallas_call(functools.partial(outputs_kernel, pieces), out_shape=tuple...  3.3 us

profile of v2, /device:TPU:0, one launch (start us, length us, event | category | flops | bytes accessed | tf_op | source)
XLA Modules:
  0.0 133.8 jit_solution(5703259506548619864)
XLA Ops:
  0.6 129.7 %layer.1 = (bf16[2,4,2,512,512]{4,3,2,1,0:T(8,128)(2,1)}, bf16[2,4,2,512,576]{4,3,2,1,0:T(8,128)(2,1)}, bf16[256,2,1024]{2,1,0:T(2,128)(2,1)}, f32[256,2,1024]{2...) custom-call(bf16[256,2,1024]{2,1,0:T(2,128)(2,1)} %x_own.1, s32[2,1024]{1,0:T(2,128)} %segs.1, s32[2,64]{1,0:T(2,128)} %vis.1, ...), custom_call_target="tpu_custom_call" | custom-call | tf_op jit(solution)/shard_map/layer/pallas_call | solution.py:892
  130.3 3.3 %outputs.1 = (bf16[256,2,1024]{2,1,0:T(2,128)(2,1)}, f32[256,2,1024]{2,1,0:T(2,128)}, f32[64,1024]{1,0:T(8,128)}, f32[64,1024]{1,0:T(8,128)}) custom-call(bf16[256,2,1024]{2,1,0:T(2,128)(2,1)} %get-tuple-element.8.refs_0_, f32[256,2,1024]{2,1,0:T(2,128)} %get-tuple-element.9.refs_1_, f32[64,1024]{1,0:T(8,128)} %get-tuple-element.10.refs_2_, ...), custom_call_target="tpu_custom_call" | custom-call | tf_op jit(solution)/shard_map/outputs/pallas_call | solution.py:930

commit v3 on v2

--- a/solution.py
+++ b/solution.py
@@ -221,12 +221,15 @@
         x_load.start()
         for copy in loads:
             copy.start()
+        pl.semaphore_wait(barrier, len(friends))
+        for group in wcross:
+            for copy in group:
+                copy.start()
         x_load.wait()
         for r in range(batch):
             xbuf[r, 0, core] = xraw[:, r, :]
-        pl.semaphore_wait(barrier, len(friends))
         x_pair.start()
-        for group in wcross + cross + [extras]:
+        for group in cross + [extras]:
             for copy in group:
                 copy.start()
         for copy in shards + far_loads:

time: 134 us -> 132 us (0.985)
  Pallas kernels: 133 us -> 131 us
    pallas_call x1, Pallas kernels: 130 us -> 128 us  [layer_call(): pl.pallas_call(functools.partial(layer_kernel, rows, chips), out_shape=sh...]
where the time goes in v3:
time: 132 us
  Pallas kernels  131 us (99%)
    pallas_call x1, Pallas kernels, layer_call(): pl.pallas_call(functools.partial(layer_kernel, rows, chips), out_shape=sh...  128 us
    pallas_call x1, Pallas kernels, outputs_call(): pl.pallas_call(functools.partial(outputs_kernel, pieces), out_shape=tuple...  3.3 us

profile of v3, /device:TPU:0, one launch (start us, length us, event | category | flops | bytes accessed | tf_op | source)
XLA Modules:
  0.0 132.2 jit_solution(11398568591712467019)
XLA Ops:
  0.6 128.0 %layer.1 = (bf16[2,4,2,512,512]{4,3,2,1,0:T(8,128)(2,1)}, bf16[2,4,2,512,576]{4,3,2,1,0:T(8,128)(2,1)}, bf16[256,2,1024]{2,1,0:T(2,128)(2,1)}, f32[256,2,1024]{2...) custom-call(bf16[256,2,1024]{2,1,0:T(2,128)(2,1)} %x_own.1, s32[2,1024]{1,0:T(2,128)} %segs.1, s32[2,64]{1,0:T(2,128)} %vis.1, ...), custom_call_target="tpu_custom_call" | custom-call | tf_op jit(solution)/shard_map/layer/pallas_call | solution.py:895
  128.7 3.3 %outputs.1 = (bf16[256,2,1024]{2,1,0:T(2,128)(2,1)}, f32[256,2,1024]{2,1,0:T(2,128)}, f32[64,1024]{1,0:T(8,128)}, f32[64,1024]{1,0:T(8,128)}) custom-call(bf16[256,2,1024]{2,1,0:T(2,128)(2,1)} %get-tuple-element.8.refs_0_, f32[256,2,1024]{2,1,0:T(2,128)} %get-tuple-element.9.refs_1_, f32[64,1024]{1,0:T(8,128)} %get-tuple-element.10.refs_2_, ...), custom_call_target="tpu_custom_call" | custom-call | tf_op jit(solution)/shard_map/outputs/pallas_call | solution.py:933

commit v4 on v3

--- a/solution.py
+++ b/solution.py
@@ -89,7 +89,7 @@
     peers = [(row, 2 * lax.rem(chip - d + chips, chips) + core) for d in range(1, chips)]
     mats = ((w_up, up), (w_dn, dn))
     cw = (rows // 2, 3)
-    ccw = (rows // 2 - 1, 3)
+    ccw = (rows // 2 - 1, 2)
     cuts = (1, 1)
     plane = [(lax.rem(row + t, rows), wide) for t in range(1, rows)]
     back = [(row, 2 * lax.rem(chip + d, chips) + core) for d in range(1, chips)]
@@ -469,6 +469,7 @@
             acc[at] = jnp.zeros_like(z)
 
         by_rows(norm_one)
+        hop(0, cw[0] + 1)
         for copy in shards + og_loads:
             copy.wait()
 
@@ -488,7 +489,6 @@
         def _(i):
             @pl.when(i == max(tiles - 1, 0))
             def _():
-                hop(0, cw[0] + 1)
                 gathered(0)
 
             @pl.when(i == tiles)

time: 132 us -> 132 us (level)
  no operation moved by 1% of the time
where the time goes in v4:
time: 132 us
  Pallas kernels  131 us (99%)
    pallas_call x1, Pallas kernels, layer_call(): pl.pallas_call(functools.partial(layer_kernel, rows, chips), out_shape=sh...  127 us
    pallas_call x1, Pallas kernels, outputs_call(): pl.pallas_call(functools.partial(outputs_kernel, pieces), out_shape=tuple...  3.3 us

profile of v4, /device:TPU:0, one launch (start us, length us, event | category | flops | bytes accessed | tf_op | source)
XLA Modules:
  0.0 131.5 jit_solution(11810515662584657987)
XLA Ops:
  0.6 127.4 %layer.1 = (bf16[2,4,2,512,512]{4,3,2,1,0:T(8,128)(2,1)}, bf16[2,4,2,512,576]{4,3,2,1,0:T(8,128)(2,1)}, bf16[256,2,1024]{2,1,0:T(2,128)(2,1)}, f32[256,2,1024]{2...) custom-call(bf16[256,2,1024]{2,1,0:T(2,128)(2,1)} %x_own.1, s32[2,1024]{1,0:T(2,128)} %segs.1, s32[2,64]{1,0:T(2,128)} %vis.1, ...), custom_call_target="tpu_custom_call" | custom-call | tf_op jit(solution)/shard_map/layer/pallas_call | solution.py:895
  128.0 3.3 %outputs.1 = (bf16[256,2,1024]{2,1,0:T(2,128)(2,1)}, f32[256,2,1024]{2,1,0:T(2,128)}, f32[64,1024]{1,0:T(8,128)}, f32[64,1024]{1,0:T(8,128)}) custom-call(bf16[256,2,1024]{2,1,0:T(2,128)(2,1)} %get-tuple-element.8.refs_0_, f32[256,2,1024]{2,1,0:T(2,128)} %get-tuple-element.9.refs_1_, f32[64,1024]{1,0:T(8,128)} %get-tuple-element.10.refs_2_, ...), custom_call_target="tpu_custom_call" | custom-call | tf_op jit(solution)/shard_map/outputs/pallas_call | solution.py:933
